TPU v7x, 128 devices: a whole 4x4x4 slice. The times are simulated.
128 devices in a mesh: dp: 32 (over z_lo, y, x), mp: 4 (over z_hi, core).
Axes of the slice: x: 4, y: 4, z: 4 (z_hi: 2, z_lo: 2; z = z_hi * 2 + z_lo), core: 2. Of those that a mesh axis runs over, the one named last changes fastest.
Arguments:
- queries: bfloat16 [20480, 4096], P('dp', 'mp'), may hold values from -180 to 180
- keys: bfloat16 [20480, 512], P('dp', 'mp'), may hold values from -6 to 6
- values: bfloat16 [20480, 512], P('dp', 'mp'), may hold values from -6 to 6
- prompt_keys: bfloat16 [128, 512], P(None, 'mp'), may hold values from -6 to 6
- prompt_values: bfloat16 [128, 512], P(None, 'mp'), may hold values from -6 to 6
- out_weight: bfloat16 [4096, 8192], P('mp', 'dp'), may hold values from -0.09375 to 0.09375
- out_grad: bfloat16 [20480, 8192], P('dp'), may hold values from -6 to 6
- lengths: int32 [32, 8], P('dp'), may hold values from 1 to 320, 640 in all within a row
Outputs:
- mixed: bfloat16 [20480, 8192], P('dp', 'mp')
- prompt_key_grad: float32 [128, 512], P('dp', 'mp')
- prompt_value_grad: float32 [128, 512], P('dp', 'mp')
All inputs are finite; a program needn't handle non-finite values.
Results may differ from a plain program's by a relative error of at most 0.024.
Values may be sent and summed in bfloat16 or wider, within the bound.
A program may use at most 192 MiB of HBM per device.

v0:
```python
import jax
import jax.numpy as jnp
from jax import lax
from jax.sharding import PartitionSpec as P

HD = 128


rope_base = 1000000.0


def split_up(x, dim, length):
    dims = x.shape
    parts = x.reshape(*dims[:dim], length, dims[dim] // length, *dims[dim + 1 :])
    return jnp.moveaxis(parts, dim, 0)


def sum_at_owner(x, axis, dim):
    length = lax.axis_size(axis)
    parts = lax.all_to_all(split_up(x, dim, length), axis, 0, 0, tiled=True)
    return jnp.sum(parts.astype(jnp.float32), axis=0)


def sent_together(arrays, axis, dim, along):
    both = jnp.concatenate(arrays, axis=along)
    filled, at, finished = (sum_at_owner(both, axis, dim), 0, [])
    for a in arrays:
        finished.append(lax.slice_in_dim(filled, at, at + a.shape[along], axis=along))
        at += a.shape[along]
    return tuple(finished)


def doc_layout(lens, count):
    ends = jnp.cumsum(lens)
    starts = ends - lens
    index = jnp.arange(count, dtype=jnp.int32)
    segment = jnp.sum((index[:, None] >= ends[None, :]).astype(jnp.int32), axis=1)
    doc_ids = jnp.arange(lens.shape[0], dtype=jnp.int32)
    offset = jnp.sum(jnp.where(segment[:, None] == doc_ids[None, :], starts[None, :], 0), axis=1)
    return (segment, index - offset)


def rotate(field, position):
    half = HD // 2
    freq = rope_base ** (-2.0 * jnp.arange(half, dtype=jnp.float32) / HD)
    angle = position.astype(jnp.float32)[:, None] * freq[None, :]
    cosine = jnp.cos(angle)[:, None, :]
    sine = jnp.sin(angle)[:, None, :]
    first = field[..., :half].astype(jnp.float32)
    second = field[..., half:].astype(jnp.float32)
    return jnp.concatenate(
        [first * cosine - second * sine, second * cosine + first * sine], axis=-1
    ).astype(jnp.bfloat16)


def per_device(queries, keys, values, prompt_keys, prompt_values, out_weight, out_grad, lengths):
    tok_rows = queries.shape[0]
    kv_local = keys.shape[1] // HD
    groups = queries.shape[1] // HD // kv_local
    prompt_rows = prompt_keys.shape[0]
    scale = HD ** (-0.5)
    segment, position = doc_layout(lengths[0], tok_rows)
    q_rot = rotate(queries.reshape(tok_rows, kv_local * groups, HD), position).reshape(
        tok_rows, kv_local, groups, HD
    )
    k_rot = rotate(keys.reshape(tok_rows, kv_local, HD), position)
    key_all = jnp.concatenate([prompt_keys.reshape(prompt_rows, kv_local, HD), k_rot], axis=0)
    value_all = jnp.concatenate(
        [prompt_values.reshape(prompt_rows, kv_local, HD), values.reshape(tok_rows, kv_local, HD)],
        axis=0,
    )
    index = jnp.arange(tok_rows, dtype=jnp.int32)
    own = (segment[:, None] == segment[None, :]) & (index[None, :] <= index[:, None])
    key_mask = jnp.concatenate([jnp.ones((tok_rows, prompt_rows), dtype=bool), own], axis=1)
    scores = (
        jnp.einsum("tkgd,skd->kgts", q_rot, key_all, preferred_element_type=jnp.float32) * scale
    )
    scores = jnp.where(key_mask[None, None], scores, -1e30)
    shifted = jnp.exp(scores - jnp.max(scores, axis=-1, keepdims=True))
    shifted = jnp.where(key_mask[None, None], shifted, 0.0)
    probs = shifted / jnp.sum(shifted, axis=-1, keepdims=True)
    probs_b = probs.astype(jnp.bfloat16)
    attn = jnp.einsum("kgts,skd->tkgd", probs_b, value_all, preferred_element_type=jnp.float32)
    attn = attn.astype(jnp.bfloat16).reshape(tok_rows, kv_local * groups * HD)
    partial_value = jnp.dot(
        attn,
        lax.all_gather(out_weight, "dp", axis=1, tiled=True),
        preferred_element_type=jnp.float32,
    )
    grad_total = lax.dot_general(
        out_grad,
        lax.all_gather(out_weight, "dp", axis=1, tiled=True),
        (((1,), (1,)), ((), ())),
        preferred_element_type=jnp.float32,
    )
    mixed = lax.psum_scatter(
        partial_value.astype(jnp.bfloat16), "mp", scatter_dimension=1, tiled=True
    )
    grad_attn = grad_total.astype(jnp.bfloat16).reshape(tok_rows, kv_local, groups, HD)
    value_grad = jnp.einsum(
        "kgts,tkgd->skd", probs_b[..., :prompt_rows], grad_attn, preferred_element_type=jnp.float32
    )
    grad_probs = jnp.einsum(
        "tkgd,skd->kgts", grad_attn, value_all, preferred_element_type=jnp.float32
    )
    d_scores = probs * (grad_probs - jnp.sum(probs * grad_probs, axis=-1, keepdims=True)) * scale
    d_scores = d_scores.astype(jnp.bfloat16)
    key_grad = jnp.einsum(
        "kgts,tkgd->skd", d_scores[..., :prompt_rows], q_rot, preferred_element_type=jnp.float32
    )
    owned = sent_together(
        (
            key_grad.reshape(prompt_rows, kv_local * HD).astype(jnp.bfloat16),
            value_grad.reshape(prompt_rows, kv_local * HD).astype(jnp.bfloat16),
        ),
        "dp",
        0,
        1,
    )
    return (mixed, owned[0], owned[1])


def solution(mesh):
    in_specs = (
        P("dp", "mp"),
        P("dp", "mp"),
        P("dp", "mp"),
        P(None, "mp"),
        P(None, "mp"),
        P("mp", "dp"),
        P("dp", None),
        P("dp", None),
    )
    out_specs = (P("dp", "mp"), P("dp", "mp"), P("dp", "mp"))
    return jax.shard_map(
        per_device, mesh=mesh, in_specs=in_specs, out_specs=out_specs, check_vma=False
    )
```

profile of v0, /device:TPU:1, one launch (start us, length us, event | category | flops | bytes accessed | tf_op | source)
XLA Modules:
  0.0 424.6 jit_solution(10789679038603178659)
XLA Ops:
  7.2 0.0 all-gather.2.cloned.1.call-start
  7.2 0.7 all-gather.2.cloned.1.call-update
  7.9 0.0 reduce-scatter.2.cloned.1.call-start
  7.9 1.7 copy.39
  9.7 0.1 fusion.47
  9.8 0.0 copy-start.2
  9.8 0.0 copy-start.4
  9.8 0.0 copy-start.3
  9.8 0.0 copy-start.5
  9.8 0.0 copy-start.6
  9.8 1.4 copy.52
  11.3 1.4 copy.53
  12.7 0.0 copy-done.2
  12.7 0.2 copy.38
  12.9 0.0 copy-done.4
  12.9 0.1 copy.37
  13.0 0.0 copy-done.3
  13.0 0.2 copy.36
  13.2 0.0 copy-done.5
  13.2 0.1 copy.35
  13.3 0.0 copy-done.6
  13.3 0.2 reduce-window.4
  13.5 0.0 copy-start.1
  13.5 0.1 convert_reduce_fusion.1
  13.6 0.3 fusion.11
  13.8 0.1 concatenate.33
  13.9 0.1 select_reduce_fusion
  14.0 0.7 fusion.37
  14.8 1.2 multiply_cosine_fusion
  16.0 0.0 copy-done.1
  16.0 2.2 fusion.6
  18.1 7.5 %fusion = (f32[8,640]{1,0:T(8,128)S(1)}, f32[768,640,8]{1,0,2:T(8,128)}) fusion(pred[640,768]{0,1:T(8,128)(4,1)S(1)} %concatenate.33, bf16[640,8,64]{2,0,1:T(8,128)(2,1)S(1)} %get-tuple-element.6, bf16[640,8,64]{2,0,1:T(8,128)(2,1)S(1)} %get-tuple-element.5, bf16[640,1,64]{0,2,1:T(8,128)(2,1)S(1)} %get-tuple-element.10, ...), kind=kOutput, calls=%fused_computation.3 | convolution fusion | flops 1021635584 | bytes 17747968 | tf_op jit(solution)/shard_map/tkgd,skd->kgts/dot_general | solution.py:76
  25.7 9.3 %fusion.2 = f32[8,640]{1,0:T(8,128)S(1)} fusion(f32[768,640,8]{1,0,2:T(8,128)} %get-tuple-element.16, f32[8,640]{1,0:T(8,128)S(1)} %get-tuple-element.15, pred[640,768]{0,1:T(8,128)(4,1)S(1)} %concatenate.33), kind=kLoop, calls=%fused_computation.6 | loop fusion | flops 19655680 | bytes 16261120 | tf_op jit(solution)/shard_map/reduce_sum | solution.py:81
  35.0 203.2 %all-gather.2.cloned.1.call-done = bf16[1024,8192]{1,0:T(8,128)(2,1)} async-done(((bf16[1024,256]{1,0:T(8,128)(2,1)}), bf16[1024,8192]{1,0:T(8,128)(2,1)}) %all-gather.2.cloned.1.call-update) | async-done | bytes 16777232 | tf_op jit(solution)/shard_map/all_gather | solution.py:87
  238.2 17.4 %convolution_convert_fusion.1 = bf16[640,1024]{1,0:T(8,128)(2,1)} fusion(bf16[640,8192]{1,0:T(8,128)(2,1)} %param.14, bf16[1024,8192]{1,0:T(8,128)(2,1)} %all-gather.2.cloned.1.call-done), kind=kOutput, calls=%fused_computation.25 | convolution fusion | flops 10738073600 | bytes 28573696 | tf_op jit(solution)/shard_map/dot_general | solution.py:90
  255.6 17.4 %multiply_reduce_fusion = (f32[8,640]{1,0:T(8,128)S(1)}, f32[1,8,640,768]{2,3,1,0:T(8,128)}, f32[1,8,640,768]{2,3,1,0:T(8,128)}) fusion(f32[8,640]{1,0:T(8,128)S(1)} %fusion.2, f32[8,640]{1,0:T(8,128)S(1)} %get-tuple-element.15, f32[768,640,8]{1,0,2:T(8,128)} %get-tuple-element.16, pred[640,768]{0,1:T(8,128)(4,1)S(1)} %concatenate.33, ...), kind=kOutput, calls=%fused_computation.1 | convolution fusion | flops 1034546176 | bytes 49246208 | tf_op jit(solution)/shard_map/tkgd,skd->kgts/dot_general | solution.py:103
  273.0 9.4 %convert_element_type.92 = bf16[1,8,640,768]{2,3,1,0:T(8,128)(2,1)} convert(f32[1,8,640,768]{2,3,1,0:T(8,128)} %get-tuple-element.4) | non-fusion elementwise | flops 3932160 | bytes 23592960 | tf_op jit(solution)/shard_map/convert_element_type | solution.py:82
  282.4 4.4 %fusion.12 = bf16[128,8,640]{2,0,1:T(8,128)(2,1)S(1)} fusion(bf16[1,8,640,768]{2,3,1,0:T(8,128)(2,1)} %convert_element_type.92, bf16[640,1,128]{0,2,1:T(8,128)(2,1)S(1)} %bitcast.106, bf16[128,1,128]{0,2,1:T(8,128)(2,1)S(1)} %bitcast.108), kind=kOutput, calls=%fused_computation.24 | convolution fusion | flops 1007681536 | bytes 9371648 | tf_op jit(solution)/shard_map/kgts,skd->tkgd/dot_general | solution.py:83
  286.8 19.5 %convolution_convert_fusion = bf16[640,8192]{1,0:T(8,128)(2,1)} fusion(bf16[640,1024]{0,1:T(8,128)(2,1)S(1)} %bitcast.102, bf16[1024,8192]{1,0:T(8,128)(2,1)} %all-gather.2.cloned.1.call-done), kind=kOutput, calls=%fused_computation.4 | convolution fusion | flops 10742661120 | bytes 28573696 | tf_op jit(solution)/shard_map/dot_general | solution.py:85
  306.4 0.0 reduce-scatter.2.cloned.1.call-update
  306.4 2.5 slice_bitcast_fusion
  308.9 2.8 copy.46
  311.7 0.0 copy-start
  311.7 1.8 copy.55
  313.5 0.0 copy-done
  313.5 0.6 fusion.23
  314.1 3.7 fusion.24
  317.8 14.4 %all_to_all.5 = bf16[32,4,256]{2,1,0:T(4,128)(2,1)S(1)} all-to-all(bf16[32,4,256]{2,1,0:T(4,128)(2,1)S(1)} %pad_maximum_fusion.3), channel_id=1, replica_groups=mesh['dp'=32,'mp'=4] {'dp'}, dimensions={0} | all-to-all | bytes 131072 | tf_op jit(solution)/shard_map/all_to_all | solution.py:20
  332.2 0.1 convert_reduce_fusion
  332.3 0.6 fusion.48
  332.9 84.9 %reduce-scatter.2.cloned.1.call-done = bf16[640,2048]{1,0:T(8,128)(2,1)} async-done(((bf16[640,8192]{1,0:T(8,128)(2,1)}), bf16[640,2048]{1,0:T(8,128)(2,1)}) %reduce-scatter.2.cloned.1.call-update) | async-done | bytes 2621456 | tf_op jit(solution)/shard_map/reduce_scatter | solution.py:96
  (4 shorter events, 0.1 us)
Async XLA Ops:
  7.2 231.0 %all-gather.2.cloned.1.call-start = ((), (), s32[]{:S(2)}) async-start(), calls=%async_computation.2 | async-start | bytes 17301504 | tf_op jit(solution)/shard_map/all_gather | solution.py:87
  7.9 409.9 %reduce-scatter.2.cloned.1.call-start = ((), (), s32[]{:S(2)}) async-start(), calls=%async_computation.3 | async-start | bytes 13107200 | tf_op jit(solution)/shard_map/reduce_scatter | solution.py:96
  9.8 2.9 copy-start.2
  9.8 3.1 copy-start.4
  9.8 3.2 copy-start.3
  9.8 3.3 copy-start.5
  9.8 3.4 copy-start.6
  13.5 2.5 copy-start.1
  311.7 1.8 copy-start
Sparse Core Ops, SparseCore 0:
  9.6 228.5 all-gather.1
  306.5 111.1 reduce-scatter.1
where the time goes:
time: 425 us
  waiting for transfers between devices  289 us (68%)
  matrix products  70.5 us (17%)
  other arithmetic  23.5 us (6%)
  blocking collectives  14.4 us (3%)
  between operations  14.3 us (3%)
  local copies, waits for them, and re-layouts  13 us (3%)
    all_gather x1, waiting for transfers between devices, per_device(): lax.all_gather(out_weight, 'dp', axis=1, tiled=True)  203 us
    reduce_scatter x1, waiting for transfers between devices, per_device(): lax.psum_scatter(partial_value.astype(jnp.bfloat16), 'mp', scatter_dimens...  84.9 us
    dot_general x1, matrix products, per_device(): jnp.dot(attn, lax.all_gather(out_weight, 'dp', axis=1, tiled=True), prefe...  19.5 us
    dot_general x1, matrix products, per_device(): lax.dot_general(out_grad, lax.all_gather(out_weight, 'dp', axis=1, tiled=...  17.4 us
    dot_general x1, matrix products, per_device(): jnp.einsum('tkgd,skd->kgts', grad_attn, value_all, preferred_element_type...  17.4 us
    all_to_all x1, blocking collectives, sum_at_owner(): parts = lax.all_to_all(split_up(x, dim, length), axis, 0, 0, tiled=True)  14.4 us
    convert_element_type x1, other arithmetic, per_device(): probs_b = probs.astype(jnp.bfloat16)  9.41 us
    reduce_sum x1, other arithmetic, per_device(): probs = shifted / jnp.sum(shifted, axis=-1, keepdims=True)  9.28 us
  transfers between devices with their start and end apart: 2, of which 2 were waited for; matrix products, arithmetic and copies ran while one was open for 9% of the time, Pallas kernels for 0%

commit v1 on v0

v1 whole, which is shorter than its diff:
```python
import functools
import math

import jax
import jax.numpy as jnp
import numpy as np
from jax import lax
from jax.experimental import pallas as pl
from jax.experimental.pallas import tpu as pltpu
from jax.sharding import PartitionSpec as P

HD = 128
DOC_MOST = 320
ROPE_BASE = 1000000.0
TILE = 128
HALF = 512
UNIT = 256
MESH = pl.DeviceIdType.MESH
F32 = jnp.float32
BF16 = jnp.bfloat16


def pick(i, values):
    out = values[0]
    for k in range(1, len(values)):
        out = jnp.where(i == k, values[k], out)
    return out


STEPS = [
    [(0, 0, 0), (0, 1, 0), (0, -1, 0), (1, 0, 0)],
    [(0, 0, 1), (0, 0, -1), (0, 2, 0), (1, 0, 1)],
    [(1, 0, -1), (1, 1, 0), (1, -1, 0), (1, 0, 2)],
    [(0, 1, -1), (0, -1, 1), (1, -1, 1), (1, 1, -1)],
    [(0, -1, -1), (0, 2, 1), (1, -1, -1), (1, 1, 2)],
    [(0, 2, -1), (0, 1, 1), (1, -1, 2), (1, 1, 1)],
    [(0, 0, 2), (0, -1, 2), (1, 2, 0), (1, 2, -1)],
    [(0, 1, 2), (0, 2, 2), (1, 2, 1), (1, 2, 2)],
]
TICKS = [
    [(0, 1, 0), (0, -1, 0), (1, 0, 1), (1, 0, -1)],
    [(0, -1, 0), (0, 2, 0), (1, 0, -1), (1, 0, 2)],
    [(0, 2, 0), (0, 1, 0), (1, 0, 2), (1, 0, 1)],
    [(0, 0, -1), (0, -1, 1), (1, -1, 0), (1, 1, -1)],
    [(0, 1, -1), (0, 2, 1), (1, -1, 1), (1, 1, 2)],
]


def kernel(
    q_hbm, k_hbm, v_hbm, pk_hbm, pv_hbm, w_hbm, og_hbm, len_ref, freq_ref,
    out_hbm, kg_ref, vg_ref,
    wall, og, part, rbuf, zbuf, acc, attn, qrot, prob, qin, kin, kall, vall, cos_t, sin_t, start_t,
    in_sem, wsend, wrecv, csend, crecv, zsend, zrecv, osem,
):
    tok = q_hbm.shape[0]
    heads = q_hbm.shape[1] // HD
    prompt = pk_hbm.shape[0]
    n_tiles = tok // TILE
    scale = HD ** -0.5
    dp = lax.axis_index("dp")
    mp = lax.axis_index("mp")
    x0, y0, zl = dp % 4, (dp // 4) % 4, dp // 16
    zh, core = mp // 2, mp % 2

    def dpid(x, y, z):
        return z * 16 + y * 4 + x

    def pa(d):
        x = jnp.where(zl == 0, (x0 + d) % 4, x0)
        y = jnp.where(zl == 0, y0, (y0 + d) % 4)
        return (dpid(x, y, zl), mp)

    def pb(d):
        x = jnp.where(zl == 0, x0, (x0 + d) % 4)
        y = jnp.where(zl == 0, (y0 + d) % 4, y0)
        return (dpid(x, y, zl), mp)

    def slot(kind, da, db):
        x = (x0 + jnp.where(zl == 0, da, db) + 4) % 4
        y = (y0 + jnp.where(zl == 0, db, da) + 4) % 4
        t = jnp.where(kind == 0, zl, 1 - zl)
        return t * 16 + y * 4 + x

    a_up, a_dn, b_up, b_dn = pa(1), pa(3), pb(1), pb(3)
    z_peer = (dpid(x0, y0, 1 - zl), mp)
    c_peer = (dp, zh * 2 + 1 - core)
    far_peer = (dp, (1 - zh) * 2 + core)

    barrier = pltpu.get_barrier_semaphore()
    for peer in (a_up, a_dn, b_up, b_dn, z_peer, c_peer, far_peer):
        pl.semaphore_signal(barrier, inc=1, device_id=peer, device_id_type=MESH)

    me = slot(0, 0, 0)
    q_copy = pltpu.make_async_copy(q_hbm, qin, in_sem.at[0])
    k_copy = pltpu.make_async_copy(k_hbm, kin, in_sem.at[1])
    pk_copy = pltpu.make_async_copy(pk_hbm, kall.at[pl.ds(0, prompt)], in_sem.at[2])
    pv_copy = pltpu.make_async_copy(pv_hbm, vall.at[pl.ds(0, prompt)], in_sem.at[3])
    v_copy = pltpu.make_async_copy(v_hbm, vall.at[pl.ds(prompt, tok)], in_sem.at[4])
    w_copy = pltpu.make_async_copy(w_hbm, wall.at[me], in_sem.at[5])
    og_copy = pltpu.make_async_copy(og_hbm, og, in_sem.at[6])
    w_copy.start()
    for c in (k_copy, pk_copy, q_copy, pv_copy, v_copy):
        c.start()

    def rows(h):
        return pl.ds(h * HALF, HALF)

    def piece(s, h):
        return wall.at[s, rows(h)]

    def send(s, h, peer, n):
        pltpu.make_async_remote_copy(
            src_ref=piece(s, h), dst_ref=piece(s, h), send_sem=wsend.at[n], recv_sem=wrecv.at[s, h],
            device_id=peer, device_id_type=MESH,
        ).start()

    def arrived(s, h):
        pltpu.make_async_remote_copy(
            src_ref=piece(s, h), dst_ref=piece(s, h), send_sem=wsend.at[0], recv_sem=wrecv.at[s, h],
            device_id=z_peer, device_id_type=MESH,
        ).wait_recv()

    pl.semaphore_wait(barrier, 7)
    w_copy.wait()
    send(me, 0, z_peer, 0)
    send(me, 0, a_up, 1)
    send(me, 1, a_dn, 2)
    send(me, 0, b_up, 3)
    send(me, 1, b_dn, 4)
    send(me, 1, z_peer, 5)
    send(me, 1, a_up, 6)
    send(me, 0, a_dn, 7)
    send(me, 1, b_up, 8)
    send(me, 0, b_dn, 9)
    og_copy.start()

    t_col = lax.broadcasted_iota(jnp.int32, (tok, HD), 0)
    begin = jnp.zeros((tok, HD), jnp.int32)
    at = jnp.int32(0)
    for d in range(len_ref.shape[1]):
        begin = jnp.where(t_col >= at, at, begin)
        at = at + len_ref[0, d]
    start_t[...] = begin
    angle = (t_col - begin).astype(F32) * freq_ref[0:1, :]
    cos_t[...] = jnp.cos(angle)
    sin_t[...] = jnp.sin(angle) * freq_ref[1:2, :]

    def rotated(field, lo, n):
        f = field.astype(F32)
        return (f * cos_t[pl.ds(lo, n), :] + pltpu.roll(f, HD // 2, 1) * sin_t[pl.ds(lo, n), :]).astype(BF16)

    k_copy.wait()
    kall[pl.ds(prompt, tok), :] = rotated(kin[...], 0, tok)
    for c in (pk_copy, q_copy, pv_copy, v_copy):
        c.wait()
    acc[...] = jnp.zeros_like(acc)

    def attention(i):
        lo = max(0, i - (DOC_MOST + TILE - 2) // TILE) * TILE
        n = (i + 1) * TILE - lo
        r = pl.ds(i * TILE, TILE)
        nt = (((1,), (1,)), ((), ()))

        def head(h, carry):
            lanes = pl.ds(pl.multiple_of(h * HD, HD), HD)
            q = rotated(qin[r, lanes], i * TILE, TILE)
            qrot[r, lanes] = q
            s_p = lax.dot_general(q, kall[pl.ds(0, prompt), :], nt, preferred_element_type=F32)
            s_t = lax.dot_general(q, kall[pl.ds(prompt + lo, n), :], nt, preferred_element_type=F32)
            col = lax.broadcasted_iota(jnp.int32, (TILE, n), 1) + lo
            row = lax.broadcasted_iota(jnp.int32, (TILE, n), 0) + i * TILE
            seen = (col <= row) & (col >= start_t[r, 0:1])
            s_t = jnp.where(seen, s_t, -1e30)
            top = jnp.maximum(jnp.max(s_p, axis=1, keepdims=True), jnp.max(s_t, axis=1, keepdims=True))
            e_p = jnp.exp((s_p - top) * scale)
            e_t = jnp.exp((s_t - top) * scale)
            inv = 1.0 / (jnp.sum(e_p, axis=1, keepdims=True) + jnp.sum(e_t, axis=1, keepdims=True))
            o = jnp.dot(e_p.astype(BF16), vall[pl.ds(0, prompt), :], preferred_element_type=F32)
            o = o + jnp.dot(e_t.astype(BF16), vall[pl.ds(prompt + lo, n), :], preferred_element_type=F32)
            attn[r, lanes] = (o * inv).astype(BF16)
            prob[r, lanes] = (e_p * inv).astype(BF16)
            return carry

        lax.fori_loop(0, heads, head, 0, unroll=2)

    attention(0)
    attention(1)
    attention(2)

    arrived(slot(0, -1, 0), 0)
    send(slot(0, -1, 0), 0, a_up, 10)
    arrived(slot(0, 1, 0), 1)
    send(slot(0, 1, 0), 1, a_dn, 11)
    other = slot(1, 0, 0)
    arrived(other, 0)
    send(other, 0, b_up, 12)
    arrived(other, 1)
    send(other, 1, b_dn, 13)
    send(other, 1, b_up, 14)
    send(other, 0, b_dn, 15)
    send(other, 0, a_up, 16)
    send(other, 1, a_dn, 17)
    send(other, 1, a_up, 18)
    send(other, 0, a_dn, 19)
    attention(3)
    attention(4)
    arrived(slot(1, 0, -1), 0)
    send(slot(1, 0, -1), 0, b_up, 20)
    arrived(slot(1, 0, 1), 1)
    send(slot(1, 0, 1), 1, b_dn, 21)
    og_copy.wait()

    def slot_of(step, table, j):
        kind = 0 if j < 2 else 1
        return slot(kind, pick(step, [t[j][1] for t in table]), pick(step, [t[j][2] for t in table]))

    def tick(t):
        n = 22 + 8 * t
        up, dn = slot_of(t, TICKS, 0), slot_of(t, TICKS, 1)
        up2, dn2 = slot_of(t, TICKS, 2), slot_of(t, TICKS, 3)
        for h in range(2):
            send(up, h, b_up, n + h)
            send(dn, h, b_dn, n + 2 + h)
            send(up2, h, a_up, n + 4 + h)
            send(dn2, h, a_dn, n + 6 + h)

    def unit(step, j):
        i = step * 4 + j
        flat = [u for four in STEPS for u in four]
        return slot(pick(i, [u[0] for u in flat]), pick(i, [u[1] for u in flat]), pick(i, [u[2] for u in flat]))

    def index_of(s):
        return (s // 16) * 8 + ((s // 4) % 2) * 4 + s % 4

    def core_copy(s):
        n = index_of(s)
        return pltpu.make_async_remote_copy(
            src_ref=part.at[s], dst_ref=rbuf.at[n], send_sem=csend.at[n], recv_sem=crecv.at[n],
            device_id=c_peer, device_id_type=MESH,
        )

    def far_copy(s):
        n = index_of(s) % 8
        return pltpu.make_async_remote_copy(
            src_ref=part.at[s], dst_ref=zbuf.at[n], send_sem=zsend.at[n], recv_sem=zrecv.at[n],
            device_id=far_peer, device_id_type=MESH,
        )

    def process(s):
        part[s] = jnp.dot(attn[...], wall[s], preferred_element_type=F32).astype(BF16)

        @pl.when((s // 8) % 2 != core)
        def _():
            core_copy(s).start()

        g = og[:, pl.ds(pl.multiple_of(s * UNIT, UNIT), UNIT)]
        for b in range(acc.shape[1] // UNIT):
            w = wall[s, b * UNIT:(b + 1) * UNIT, :]
            acc[:, b * UNIT:(b + 1) * UNIT] += lax.dot_general(
                g, w, (((1,), (1,)), ((), ())), preferred_element_type=F32
            )

    def combine(s):
        @pl.when((s // 8) % 2 == core)
        def _():
            n = index_of(s)
            core_copy(s).wait_recv()
            part[s] = (part[s].astype(F32) + rbuf[n].astype(F32)).astype(BF16)

            @pl.when(s // 16 != zh)
            def _():
                far_copy(s).start()

    def both(s):
        arrived(s, 0)
        arrived(s, 1)

    def step_body(step, carry):
        @pl.when(step == 0)
        def _():
            arrived(slot(0, -1, 0), 1)
            arrived(slot(0, 1, 0), 0)

        @pl.when(step == 1)
        def _():
            both(slot(0, 0, 1))
            both(slot(0, 0, -1))
            both(slot(0, 2, 0))
            arrived(slot(1, 0, -1), 1)
            arrived(slot(1, 0, 1), 0)
            tick(0)

        @pl.when(step == 2)
        def _():
            both(slot(1, 1, 0))
            both(slot(1, -1, 0))
            both(slot(1, 0, 2))
            tick(1)

        @pl.when(step >= 3)
        def _():
            for j in range(4):
                both(unit(step, j))

            @pl.when(step <= 5)
            def _():
                tick(step - 1)

        def one(j, c):
            process(unit(step, j))
            return c

        lax.fori_loop(0, 4, one, 0)

        @pl.when(step > 0)
        def _():
            def two(j, c):
                combine(unit(step - 1, j))
                return c

            lax.fori_loop(0, 4, two, 0)

        return carry

    lax.fori_loop(0, 8, step_body, 0)

    def last(j, c):
        combine(unit(7, j))
        return c

    lax.fori_loop(0, 4, last, 0)

    tn = (((0,), (0,)), ((), ()))
    nt = (((1,), (1,)), ((), ()))
    kg_ref[...] = jnp.zeros_like(kg_ref)
    vg_ref[...] = jnp.zeros_like(vg_ref)

    def grads(h, c):
        lanes = pl.ds(pl.multiple_of(h * HD, HD), HD)
        g = acc[:, lanes].astype(BF16)
        p = prob[:, lanes]
        delta = jnp.sum(g.astype(F32) * attn[:, lanes].astype(F32), axis=1, keepdims=True)
        gp = lax.dot_general(g, vall[pl.ds(0, prompt), :], nt, preferred_element_type=F32)
        ds = (p.astype(F32) * (gp - delta) * scale).astype(BF16)
        kg_ref[...] += lax.dot_general(ds, qrot[:, lanes], tn, preferred_element_type=F32)
        vg_ref[...] += lax.dot_general(p, g, tn, preferred_element_type=F32)
        return c

    lax.fori_loop(0, heads, grads, 0)

    def out_copy(n):
        s = zh * 16 + core * 8 + n
        return pltpu.make_async_copy(
            part.at[s], out_hbm.at[:, pl.ds(pl.multiple_of(n * UNIT, UNIT), UNIT)], osem.at[n]
        )

    def finish(j, c):
        s = unit(j // 4, j % 4)

        @pl.when(((s // 8) % 2 == core) & (s // 16 == zh))
        def _():
            n = index_of(s) % 8
            far_copy(s).wait_recv()
            part[s] = (part[s].astype(F32) + zbuf[n].astype(F32)).astype(BF16)
            out_copy(n).start()

        return c

    lax.fori_loop(0, 32, finish, 0)

    def drain(n, c):
        pltpu.make_async_remote_copy(
            src_ref=piece(0, 0), dst_ref=piece(0, 0), send_sem=wsend.at[n], recv_sem=wrecv.at[0, 0],
            device_id=z_peer, device_id_type=MESH,
        ).wait_send()
        return c

    lax.fori_loop(0, 62, drain, 0)

    def drain_parts(s, c):
        @pl.when((s // 8) % 2 != core)
        def _():
            core_copy(s).wait_send()

        @pl.when(((s // 8) % 2 == core) & (s // 16 != zh))
        def _():
            far_copy(s).wait_send()

        return c

    lax.fori_loop(0, 32, drain_parts, 0)

    def drain_out(n, c):
        out_copy(n).wait()
        return c

    lax.fori_loop(0, 8, drain_out, 0)


def split_up(x, dim, length):
    dims = x.shape
    parts = x.reshape(*dims[:dim], length, dims[dim] // length, *dims[dim + 1:])
    return jnp.moveaxis(parts, dim, 0)


def sum_at_owner(x, axis, dim):
    length = lax.axis_size(axis)
    parts = lax.all_to_all(split_up(x, dim, length), axis, 0, 0, tiled=True)
    return jnp.sum(parts.astype(F32), axis=0)


def per_device(queries, keys, values, prompt_keys, prompt_values, out_weight, out_grad, lengths):
    tok, width = queries.shape
    prompt = prompt_keys.shape[0]
    n_dp = lax.axis_size("dp")
    half = HD // 2
    freq = ROPE_BASE ** (-2.0 * np.arange(half) / HD)
    table = np.zeros((8, HD), np.float32)
    table[0] = np.concatenate([freq, freq])
    table[1] = np.concatenate([-np.ones(half), np.ones(half)])
    anywhere = pl.BlockSpec(memory_space=pl.ANY)
    vmem = pl.BlockSpec(memory_space=pltpu.VMEM)
    dma = pltpu.SemaphoreType.DMA
    mixed, key_grad, value_grad = pl.pallas_call(
        kernel,
        out_shape=(
            jax.ShapeDtypeStruct((tok, 8 * UNIT), BF16),
            jax.ShapeDtypeStruct((prompt, HD), F32),
            jax.ShapeDtypeStruct((prompt, HD), F32),
        ),
        in_specs=[anywhere] * 7 + [pl.BlockSpec(memory_space=pltpu.SMEM), vmem],
        out_specs=(anywhere, vmem, vmem),
        scratch_shapes=[
            pltpu.VMEM((n_dp, width, UNIT), BF16),
            pltpu.VMEM((tok, n_dp * UNIT), BF16),
            pltpu.VMEM((n_dp, tok, UNIT), BF16),
            pltpu.VMEM((16, tok, UNIT), BF16),
            pltpu.VMEM((8, tok, UNIT), BF16),
            pltpu.VMEM((tok, width), F32),
            pltpu.VMEM((tok, width), BF16),
            pltpu.VMEM((tok, width), BF16),
            pltpu.VMEM((tok, width), BF16),
            pltpu.VMEM((tok, width), BF16),
            pltpu.VMEM((tok, HD), BF16),
            pltpu.VMEM((prompt + tok, HD), BF16),
            pltpu.VMEM((prompt + tok, HD), BF16),
            pltpu.VMEM((tok, HD), F32),
            pltpu.VMEM((tok, HD), F32),
            pltpu.VMEM((tok, HD), jnp.int32),
            dma((7,)),
            dma((62,)),
            dma((n_dp, 2)),
            dma((16,)),
            dma((16,)),
            dma((8,)),
            dma((8,)),
            dma((8,)),
        ],
        compiler_params=pltpu.CompilerParams(
            collective_id=0, has_side_effects=True, vmem_limit_bytes=62 * 1024 * 1024
        ),
    )(queries, keys, values, prompt_keys, prompt_values, out_weight, out_grad, lengths, jnp.asarray(table))
    both = jnp.concatenate([key_grad, value_grad], axis=1).astype(BF16)
    owned = sum_at_owner(both, "dp", 0)
    return mixed, owned[:, :HD], owned[:, HD:]


def solution(mesh):
    in_specs = (
        P("dp", "mp"),
        P("dp", "mp"),
        P("dp", "mp"),
        P(None, "mp"),
        P(None, "mp"),
        P("mp", "dp"),
        P("dp", None),
        P("dp", None),
    )
    out_specs = (P("dp", "mp"), P("dp", "mp"), P("dp", "mp"))
    return jax.shard_map(
        per_device, mesh=mesh, in_specs=in_specs, out_specs=out_specs, check_vma=False
    )
```

time: 425 us -> 144 us (0.34)
  the two profiles are of different devices: /device:TPU:1 before, /device:TPU:0 now
where the time goes in v1:
time: 144 us
  Pallas kernels  116 us (81%)
  starting transfers between devices  11.6 us (8%)
  waiting for transfers between devices  8.33 us (6%)
  local copies, waits for them, and re-layouts  4.15 us (3%)
  other arithmetic  2.4 us (2%)
    pallas_call x1, Pallas kernels, per_device(): pl.pallas_call(kernel, out_shape=(jax.ShapeDtypeStruct((tok, 8 * UNIT), B...  116 us
    all_to_all x1, starting transfers between devices, sum_at_owner(): parts = lax.all_to_all(split_up(x, dim, length), axis, 0, 0, tiled=True)  11.6 us
    all_to_all x1, waiting for transfers between devices, sum_at_owner(): parts = lax.all_to_all(split_up(x, dim, length), axis, 0, 0, tiled=True)  8.33 us
    unnamed x1, local copies, waits for them, and re-layouts  3.56 us
  transfers between devices with their start and end apart: 1, of which 1 were waited for; matrix products, arithmetic and copies ran while one was open for 0% of the time, Pallas kernels for 0%

profile of v1, /device:TPU:0, one launch (start us, length us, event | category | flops | bytes accessed | tf_op | source)
XLA Modules:
  0.0 143.5 jit_solution(5719037447747335568)
XLA Ops:
  0.6 116.3 %shard_map.112 = (bf16[640,2048]{1,0:T(8,128)(2,1)}, f32[128,128]{1,0:T(8,128)}, f32[128,128]{1,0:T(8,128)}) custom-call(bf16[640,1024]{1,0:T(8,128)(2,1)} %q_hbm.1, bf16[640,128]{1,0:T(8,128)(2,1)} %k_hbm.1, bf16[640,128]{1,0:T(8,128)(2,1)} %v_hbm.1, bf16[128,128]{1,0:T(8,128)(2,1)} %pk_hbm.1, bf16[128,128]{1,0:T(8,128)(2,1)} %pv_hbm.1, ...), custom_call_target="tpu_custom_call" | custom-call | tf_op jit(solution)/shard_map/pallas_call | solution.py:424
  117.0 0.8 convert.8
  117.8 0.8 convert.9
  118.7 0.7 pad_maximum_fusion
  119.3 11.6 %all-to-all-start = ((bf16[32,4,256]{2,1,0:T(4,128)(2,1)}), bf16[32,4,256]{2,1,0:T(4,128)(2,1)S(1)}, u32[]{:S(2)}, u32[]{:S(2)}) async-start(bf16[32,4,256]{2,1,0:T(4,128)(2,1)} %pad_maximum_fusion), calls=%async_computation | async-start | bytes 131072 | tf_op jit(solution)/shard_map/all_to_all | solution.py:408
  131.0 8.3 %all-to-all-done = bf16[32,4,256]{2,1,0:T(4,128)(2,1)S(1)} async-done(((bf16[32,4,256]{2,1,0:T(4,128)(2,1)}), bf16[32,4,256]{2,1,0:T(4,128)(2,1)S(1)}, u32[]{:S(2)}, u32[]{:S(2)}) %all-to-all-start) | async-done | bytes 65568 | tf_op jit(solution)/shard_map/all_to_all | solution.py:408
  139.3 0.1 convert_reduce_fusion
  139.4 0.6 fusion
  139.9 3.6 %copy.13 = bf16[640,2048]{1,0:T(8,128)(2,1)} copy(bf16[640,2048]{1,0:T(8,128)(2,1)} %get-tuple-element.14) | data formatting | bytes 5242880
Async XLA Ops:
  119.3 20.0 %all-to-all-start = ((bf16[32,4,256]{2,1,0:T(4,128)(2,1)}), bf16[32,4,256]{2,1,0:T(4,128)(2,1)S(1)}, u32[]{:S(2)}, u32[]{:S(2)}) async-start(bf16[32,4,256]{2,1,0:T(4,128)(2,1)} %pad_maximum_fusion), calls=%async_computation | async-start | bytes 131072 | tf_op jit(solution)/shard_map/all_to_all | solution.py:408

commit v2 on v1

--- a/solution.py
+++ b/solution.py
@@ -48,9 +48,9 @@
 
 def kernel(
     q_hbm, k_hbm, v_hbm, pk_hbm, pv_hbm, w_hbm, og_hbm, len_ref, freq_ref,
-    out_hbm, kg_ref, vg_ref,
-    wall, og, part, rbuf, zbuf, acc, attn, qrot, prob, qin, kin, kall, vall, cos_t, sin_t, start_t,
-    in_sem, wsend, wrecv, csend, crecv, zsend, zrecv, osem,
+    own_hbm, far_hbm, g_out,
+    wall, og, part, rbuf, kg, vg, gsend, grecv, acc, attn, qrot, prob, qin, kin, kall, vall, cos_t, sin_t, start_t,
+    in_sem, wsend, wrecv, csend, crecv, zsend, zrecv, osem, gssem, grsem,
 ):
     tok = q_hbm.shape[0]
     heads = q_hbm.shape[1] // HD
@@ -108,6 +108,12 @@
     def piece(s, h):
         return wall.at[s, rows(h)]
 
+    def send_own(h, peer, n):
+        pltpu.make_async_remote_copy(
+            src_ref=w_hbm.at[rows(h)], dst_ref=piece(me, h), send_sem=wsend.at[n], recv_sem=wrecv.at[me, h],
+            device_id=peer, device_id_type=MESH,
+        ).start()
+
     def send(s, h, peer, n):
         pltpu.make_async_remote_copy(
             src_ref=piece(s, h), dst_ref=piece(s, h), send_sem=wsend.at[n], recv_sem=wrecv.at[s, h],
@@ -121,17 +127,16 @@
         ).wait_recv()
 
     pl.semaphore_wait(barrier, 7)
-    w_copy.wait()
-    send(me, 0, z_peer, 0)
-    send(me, 0, a_up, 1)
-    send(me, 1, a_dn, 2)
-    send(me, 0, b_up, 3)
-    send(me, 1, b_dn, 4)
-    send(me, 1, z_peer, 5)
-    send(me, 1, a_up, 6)
-    send(me, 0, a_dn, 7)
-    send(me, 1, b_up, 8)
-    send(me, 0, b_dn, 9)
+    send_own(0, z_peer, 0)
+    send_own(0, a_up, 1)
+    send_own(1, a_dn, 2)
+    send_own(0, b_up, 3)
+    send_own(1, b_dn, 4)
+    send_own(1, z_peer, 5)
+    send_own(1, a_up, 6)
+    send_own(0, a_dn, 7)
+    send_own(1, b_up, 8)
+    send_own(0, b_dn, 9)
     og_copy.start()
 
     t_col = lax.broadcasted_iota(jnp.int32, (tok, HD), 0)
@@ -151,7 +156,7 @@
 
     k_copy.wait()
     kall[pl.ds(prompt, tok), :] = rotated(kin[...], 0, tok)
-    for c in (pk_copy, q_copy, pv_copy, v_copy):
+    for c in (pk_copy, q_copy, pv_copy, v_copy, w_copy):
         c.wait()
     acc[...] = jnp.zeros_like(acc)
 
@@ -225,7 +230,7 @@
             send(dn2, h, a_dn, n + 6 + h)
 
     def unit(step, j):
-        i = step * 4 + j
+        i = step * 4 + jnp.where((step >= 3) & (zl == zh), (j + 2) % 4, j)
         flat = [u for four in STEPS for u in four]
         return slot(pick(i, [u[0] for u in flat]), pick(i, [u[1] for u in flat]), pick(i, [u[2] for u in flat]))
 
@@ -242,9 +247,16 @@
     def far_copy(s):
         n = index_of(s) % 8
         return pltpu.make_async_remote_copy(
-            src_ref=part.at[s], dst_ref=zbuf.at[n], send_sem=zsend.at[n], recv_sem=zrecv.at[n],
+            src_ref=part.at[s], dst_ref=far_hbm.at[:, columns(n)], send_sem=zsend.at[n], recv_sem=zrecv.at[n],
             device_id=far_peer, device_id_type=MESH,
         )
+
+    def columns(n):
+        return pl.ds(pl.multiple_of(n * UNIT, UNIT), UNIT)
+
+    def own_copy(s):
+        n = index_of(s) % 8
+        return pltpu.make_async_copy(part.at[s], own_hbm.at[:, columns(n)], osem.at[n])
 
     def process(s):
         part[s] = jnp.dot(attn[...], wall[s], preferred_element_type=F32).astype(BF16)
@@ -271,6 +283,10 @@
             def _():
                 far_copy(s).start()
 
+            @pl.when(s // 16 == zh)
+            def _():
+                own_copy(s).start()
+
     def both(s):
         arrived(s, 0)
         arrived(s, 1)
@@ -297,43 +313,37 @@
             both(slot(1, 0, 2))
             tick(1)
 
-        @pl.when(step >= 3)
+        @pl.when((step >= 3) & (step <= 5))
         def _():
             for j in range(4):
                 both(unit(step, j))
-
-            @pl.when(step <= 5)
+            tick(step - 1)
+
+        def one(j, c):
+            s = unit(step, j)
+
+            @pl.when(step >= 6)
             def _():
-                tick(step - 1)
-
-        def one(j, c):
-            process(unit(step, j))
+                both(s)
+
+            process(s)
+
+            @pl.when(j > 0)
+            def _():
+                combine(unit(step, j - 1))
+
             return c
 
         lax.fori_loop(0, 4, one, 0)
-
-        @pl.when(step > 0)
-        def _():
-            def two(j, c):
-                combine(unit(step - 1, j))
-                return c
-
-            lax.fori_loop(0, 4, two, 0)
-
+        combine(unit(step, 3))
         return carry
 
     lax.fori_loop(0, 8, step_body, 0)
-
-    def last(j, c):
-        combine(unit(7, j))
-        return c
-
-    lax.fori_loop(0, 4, last, 0)
 
     tn = (((0,), (0,)), ((), ()))
     nt = (((1,), (1,)), ((), ()))
-    kg_ref[...] = jnp.zeros_like(kg_ref)
-    vg_ref[...] = jnp.zeros_like(vg_ref)
+    kg[...] = jnp.zeros_like(kg)
+    vg[...] = jnp.zeros_like(vg)
 
     def grads(h, c):
         lanes = pl.ds(pl.multiple_of(h * HD, HD), HD)
@@ -342,31 +352,29 @@
         delta = jnp.sum(g.astype(F32) * attn[:, lanes].astype(F32), axis=1, keepdims=True)
         gp = lax.dot_general(g, vall[pl.ds(0, prompt), :], nt, preferred_element_type=F32)
         ds = (p.astype(F32) * (gp - delta) * scale).astype(BF16)
-        kg_ref[...] += lax.dot_general(ds, qrot[:, lanes], tn, preferred_element_type=F32)
-        vg_ref[...] += lax.dot_general(p, g, tn, preferred_element_type=F32)
+        kg[...] += lax.dot_general(ds, qrot[:, lanes], tn, preferred_element_type=F32)
+        vg[...] += lax.dot_general(p, g, tn, preferred_element_type=F32)
         return c
 
     lax.fori_loop(0, heads, grads, 0)
 
-    def out_copy(n):
-        s = zh * 16 + core * 8 + n
-        return pltpu.make_async_copy(
-            part.at[s], out_hbm.at[:, pl.ds(pl.multiple_of(n * UNIT, UNIT), UNIT)], osem.at[n]
+    n_dp = gsend.shape[0]
+    own_rows = prompt // n_dp
+    gsend[:, 0:own_rows, :] = kg[...].reshape(n_dp, own_rows, HD)
+    gsend[:, own_rows:2 * own_rows, :] = vg[...].reshape(n_dp, own_rows, HD)
+
+    def grad_copy(j):
+        return pltpu.make_async_remote_copy(
+            src_ref=gsend.at[(dp + j) % n_dp], dst_ref=grecv.at[dp], send_sem=gssem.at[j], recv_sem=grsem.at[dp],
+            device_id=((dp + j) % n_dp, mp), device_id_type=MESH,
         )
 
-    def finish(j, c):
-        s = unit(j // 4, j % 4)
-
-        @pl.when(((s // 8) % 2 == core) & (s // 16 == zh))
-        def _():
-            n = index_of(s) % 8
-            far_copy(s).wait_recv()
-            part[s] = (part[s].astype(F32) + zbuf[n].astype(F32)).astype(BF16)
-            out_copy(n).start()
-
+    def grad_send(j, c):
+        grad_copy(j).start()
         return c
 
-    lax.fori_loop(0, 32, finish, 0)
+    lax.fori_loop(1, n_dp, grad_send, 0)
+    grecv[dp] = gsend[dp]
 
     def drain(n, c):
         pltpu.make_async_remote_copy(
@@ -382,37 +390,44 @@
         def _():
             core_copy(s).wait_send()
 
-        @pl.when(((s // 8) % 2 == core) & (s // 16 != zh))
-        def _():
-            far_copy(s).wait_send()
+        @pl.when(((s // 8) % 2 == core) & (s // 16 == zh))
+        def _():
+            own_copy(s).wait()
 
         return c
 
-    lax.fori_loop(0, 32, drain_parts, 0)
-
-    def drain_out(n, c):
-        out_copy(n).wait()
+    lax.fori_loop(0, n_dp, drain_parts, 0)
+
+    def grad_wait(j, c):
+        src = (dp + j) % n_dp
+        pltpu.make_async_remote_copy(
+            src_ref=gsend.at[src], dst_ref=grecv.at[src], send_sem=gssem.at[j], recv_sem=grsem.at[src],
+            device_id=(src, mp), device_id_type=MESH,
+        ).wait()
         return c
 
-    lax.fori_loop(0, 8, drain_out, 0)
-
-
-def split_up(x, dim, length):
-    dims = x.shape
-    parts = x.reshape(*dims[:dim], length, dims[dim] // length, *dims[dim + 1:])
-    return jnp.moveaxis(parts, dim, 0)
-
-
-def sum_at_owner(x, axis, dim):
-    length = lax.axis_size(axis)
-    parts = lax.all_to_all(split_up(x, dim, length), axis, 0, 0, tiled=True)
-    return jnp.sum(parts.astype(F32), axis=0)
+    lax.fori_loop(1, n_dp, grad_wait, 0)
+    g_out[...] = jnp.sum(grecv[...], axis=0)
+
+    def far_wait(n, c):
+        far_copy((1 - zh) * 16 + core * 8 + n).wait()
+        return c
+
+    lax.fori_loop(0, 8, far_wait, 0)
+
+
+def finish(own_ref, far_ref, g_ref, out_ref, kg_ref, vg_ref):
+    out_ref[...] = (own_ref[...].astype(F32) + far_ref[...].astype(F32)).astype(BF16)
+    n = kg_ref.shape[0]
+    kg_ref[...] = g_ref[0:n, :]
+    vg_ref[...] = g_ref[n:2 * n, :]
 
 
 def per_device(queries, keys, values, prompt_keys, prompt_values, out_weight, out_grad, lengths):
     tok, width = queries.shape
     prompt = prompt_keys.shape[0]
     n_dp = lax.axis_size("dp")
+    own_rows = prompt // n_dp
     half = HD // 2
     freq = ROPE_BASE ** (-2.0 * np.arange(half) / HD)
     table = np.zeros((8, HD), np.float32)
@@ -421,21 +436,24 @@
     anywhere = pl.BlockSpec(memory_space=pl.ANY)
     vmem = pl.BlockSpec(memory_space=pltpu.VMEM)
     dma = pltpu.SemaphoreType.DMA
-    mixed, key_grad, value_grad = pl.pallas_call(
+    own, far, grad = pl.pallas_call(
         kernel,
         out_shape=(
             jax.ShapeDtypeStruct((tok, 8 * UNIT), BF16),
-            jax.ShapeDtypeStruct((prompt, HD), F32),
-            jax.ShapeDtypeStruct((prompt, HD), F32),
+            jax.ShapeDtypeStruct((tok, 8 * UNIT), BF16),
+            jax.ShapeDtypeStruct((2 * own_rows, HD), F32),
         ),
         in_specs=[anywhere] * 7 + [pl.BlockSpec(memory_space=pltpu.SMEM), vmem],
-        out_specs=(anywhere, vmem, vmem),
+        out_specs=(anywhere, anywhere, vmem),
         scratch_shapes=[
             pltpu.VMEM((n_dp, width, UNIT), BF16),
             pltpu.VMEM((tok, n_dp * UNIT), BF16),
             pltpu.VMEM((n_dp, tok, UNIT), BF16),
             pltpu.VMEM((16, tok, UNIT), BF16),
-            pltpu.VMEM((8, tok, UNIT), BF16),
+            pltpu.VMEM((prompt, HD), F32),
+            pltpu.VMEM((prompt, HD), F32),
+            pltpu.VMEM((n_dp, 2 * own_rows, HD), F32),
+            pltpu.VMEM((n_dp, 2 * own_rows, HD), F32),
             pltpu.VMEM((tok, width), F32),
             pltpu.VMEM((tok, width), BF16),
             pltpu.VMEM((tok, width), BF16),
@@ -455,14 +473,27 @@
             dma((8,)),
             dma((8,)),
             dma((8,)),
+            dma((n_dp,)),
+            dma((n_dp,)),
         ],
         compiler_params=pltpu.CompilerParams(
             collective_id=0, has_side_effects=True, vmem_limit_bytes=62 * 1024 * 1024
         ),
     )(queries, keys, values, prompt_keys, prompt_values, out_weight, out_grad, lengths, jnp.asarray(table))
-    both = jnp.concatenate([key_grad, value_grad], axis=1).astype(BF16)
-    owned = sum_at_owner(both, "dp", 0)
-    return mixed, owned[:, :HD], owned[:, HD:]
+    block = 2 * TILE if tok % (2 * TILE) == 0 else TILE
+    wide = pl.BlockSpec((block, 8 * UNIT), lambda i: (i, 0))
+    few = pl.BlockSpec((own_rows, HD), lambda i: (0, 0))
+    return pl.pallas_call(
+        finish,
+        grid=(tok // block,),
+        out_shape=(
+            jax.ShapeDtypeStruct((tok, 8 * UNIT), BF16),
+            jax.ShapeDtypeStruct((own_rows, HD), F32),
+            jax.ShapeDtypeStruct((own_rows, HD), F32),
+        ),
+        in_specs=[wide, wide, pl.BlockSpec((2 * own_rows, HD), lambda i: (0, 0))],
+        out_specs=(wide, few, few),
+    )(own, far, grad)
 
 
 def solution(mesh):

time: 144 us -> 121 us (0.84)
  the two profiles are of different devices: /device:TPU:0 before, /device:TPU:1 now
where the time goes in v2:
time: 121 us
  Pallas kernels  120 us (99%)
    pallas_call x1, Pallas kernels, per_device(): pl.pallas_call(kernel, out_shape=(jax.ShapeDtypeStruct((tok, 8 * UNIT), B...  114 us
    pallas_call x1, Pallas kernels, per_device(): pl.pallas_call(finish, grid=(tok // block,), out_shape=(jax.ShapeDtypeStr...  5.68 us

profile of v2, /device:TPU:1, one launch (start us, length us, event | category | flops | bytes accessed | tf_op | source)
XLA Modules:
  0.0 120.8 jit_solution(867711690897183720)
XLA Ops:
  0.6 114.5 %shard_map.112 = (bf16[640,2048]{1,0:T(8,128)(2,1)}, bf16[640,2048]{1,0:T(8,128)(2,1)}, f32[8,128]{1,0:T(8,128)}) custom-call(bf16[640,1024]{1,0:T(8,128)(2,1)} %q_hbm.1, bf16[640,128]{1,0:T(8,128)(2,1)} %k_hbm.1, bf16[640,128]{1,0:T(8,128)(2,1)} %v_hbm.1, bf16[128,128]{1,0:T(8,128)(2,1)} %pk_hbm.1, bf16[128,128]{1,0:T(8,128)(2,1)} %pv_hbm.1, ...), custom_call_target="tpu_custom_call" | custom-call | tf_op jit(solution)/shard_map/pallas_call | solution.py:439
  115.1 5.7 %shard_map.113 = (bf16[640,2048]{1,0:T(8,128)(2,1)}, f32[4,128]{1,0:T(4,128)}, f32[4,128]{1,0:T(4,128)}) custom-call(bf16[640,2048]{1,0:T(8,128)(2,1)} %get-tuple-element.6.own_ref, bf16[640,2048]{1,0:T(8,128)(2,1)} %get-tuple-element.7.far_ref, f32[8,128]{1,0:T(8,128)} %get-tuple-element.8.g_ref), custom_call_target="tpu_custom_call" | custom-call | tf_op jit(solution)/shard_map/pallas_call | solution.py:486

commit v3 on v2

--- a/solution.py
+++ b/solution.py
@@ -48,9 +48,9 @@
 
 def kernel(
     q_hbm, k_hbm, v_hbm, pk_hbm, pv_hbm, w_hbm, og_hbm, len_ref, freq_ref,
-    own_hbm, far_hbm, g_out,
-    wall, og, part, rbuf, kg, vg, gsend, grecv, acc, attn, qrot, prob, qin, kin, kall, vall, cos_t, sin_t, start_t,
-    in_sem, wsend, wrecv, csend, crecv, zsend, zrecv, osem, gssem, grsem,
+    out_ref, kg_out, vg_out,
+    wall, og, part, rbuf, zbuf, early, kg, vg, gsend, grecv, acc, attn, qrot, prob_t, qin, kin, kall, vall, cos_t, sin_t, start_t,
+    in_sem, wsend, wrecv, csend, crecv, zsend, zrecv, gssem, grsem,
 ):
     tok = q_hbm.shape[0]
     heads = q_hbm.shape[1] // HD
@@ -183,7 +183,7 @@
             o = jnp.dot(e_p.astype(BF16), vall[pl.ds(0, prompt), :], preferred_element_type=F32)
             o = o + jnp.dot(e_t.astype(BF16), vall[pl.ds(prompt + lo, n), :], preferred_element_type=F32)
             attn[r, lanes] = (o * inv).astype(BF16)
-            prob[r, lanes] = (e_p * inv).astype(BF16)
+            prob_t[lanes, r] = jnp.transpose(e_p * inv).astype(BF16)
             return carry
 
         lax.fori_loop(0, heads, head, 0, unroll=2)
@@ -247,31 +247,32 @@
     def far_copy(s):
         n = index_of(s) % 8
         return pltpu.make_async_remote_copy(
-            src_ref=part.at[s], dst_ref=far_hbm.at[:, columns(n)], send_sem=zsend.at[n], recv_sem=zrecv.at[n],
+            src_ref=part.at[s], dst_ref=zbuf.at[n], send_sem=zsend.at[n], recv_sem=zrecv.at[n],
             device_id=far_peer, device_id_type=MESH,
         )
 
     def columns(n):
         return pl.ds(pl.multiple_of(n * UNIT, UNIT), UNIT)
 
-    def own_copy(s):
-        n = index_of(s) % 8
-        return pltpu.make_async_copy(part.at[s], own_hbm.at[:, columns(n)], osem.at[n])
-
-    def process(s):
-        part[s] = jnp.dot(attn[...], wall[s], preferred_element_type=F32).astype(BF16)
-
+    def hand_over(s):
         @pl.when((s // 8) % 2 != core)
         def _():
             core_copy(s).start()
 
-        g = og[:, pl.ds(pl.multiple_of(s * UNIT, UNIT), UNIT)]
-        for b in range(acc.shape[1] // UNIT):
+    def add_grad(s, half):
+        g = og[:, columns(s)]
+        for b in range(half * HALF // UNIT, (half + 1) * HALF // UNIT):
             w = wall[s, b * UNIT:(b + 1) * UNIT, :]
             acc[:, b * UNIT:(b + 1) * UNIT] += lax.dot_general(
                 g, w, (((1,), (1,)), ((), ())), preferred_element_type=F32
             )
 
+    def process(s):
+        part[s] = jnp.dot(attn[...], wall[s], preferred_element_type=F32).astype(BF16)
+        hand_over(s)
+        add_grad(s, 0)
+        add_grad(s, 1)
+
     def combine(s):
         @pl.when((s // 8) % 2 == core)
         def _():
@@ -282,10 +283,6 @@
             @pl.when(s // 16 != zh)
             def _():
                 far_copy(s).start()
-
-            @pl.when(s // 16 == zh)
-            def _():
-                own_copy(s).start()
 
     def both(s):
         arrived(s, 0)
@@ -322,7 +319,7 @@
         def one(j, c):
             s = unit(step, j)
 
-            @pl.when(step >= 6)
+            @pl.when(step == 6)
             def _():
                 both(s)
 
@@ -338,43 +335,95 @@
         combine(unit(step, 3))
         return carry
 
-    lax.fori_loop(0, 8, step_body, 0)
-
-    tn = (((0,), (0,)), ((), ()))
+    lax.fori_loop(0, 7, step_body, 0)
+
+    nn = (((1,), (0,)), ((), ()))
     nt = (((1,), (1,)), ((), ()))
     kg[...] = jnp.zeros_like(kg)
     vg[...] = jnp.zeros_like(vg)
 
     def grads(h, c):
         lanes = pl.ds(pl.multiple_of(h * HD, HD), HD)
-        g = acc[:, lanes].astype(BF16)
-        p = prob[:, lanes]
-        delta = jnp.sum(g.astype(F32) * attn[:, lanes].astype(F32), axis=1, keepdims=True)
-        gp = lax.dot_general(g, vall[pl.ds(0, prompt), :], nt, preferred_element_type=F32)
+        g32 = acc[:, lanes].astype(BF16).astype(F32)
+        g = g32.astype(BF16)
+        p = prob_t[lanes, :]
+        weighed = (g32 * attn[:, lanes].astype(F32)).astype(BF16)
+        delta = lax.dot_general(jnp.ones((8, HD), BF16), weighed, nt, preferred_element_type=F32)[0:1, :]
+        gp = lax.dot_general(vall[pl.ds(0, prompt), :], g, nt, preferred_element_type=F32)
         ds = (p.astype(F32) * (gp - delta) * scale).astype(BF16)
-        kg[...] += lax.dot_general(ds, qrot[:, lanes], tn, preferred_element_type=F32)
-        vg[...] += lax.dot_general(p, g, tn, preferred_element_type=F32)
-        return c
-
-    lax.fori_loop(0, heads, grads, 0)
+        kg[...] += lax.dot_general(ds, qrot[:, lanes], nn, preferred_element_type=F32)
+        vg[...] += lax.dot_general(p, g, nn, preferred_element_type=F32)
+        return c
+
+    def first_half(j, c):
+        s = unit(7, j)
+        arrived(s, 0)
+        early[j] = jnp.dot(attn[:, 0:HALF], wall[s, 0:HALF, :], preferred_element_type=F32)
+        add_grad(s, 0)
+        return c
+
+    lax.fori_loop(0, 4, first_half, 0)
+    lax.fori_loop(0, heads // 2, grads, 0)
+
+    def second_product(j, c):
+        s = unit(7, j)
+        rest = jnp.dot(attn[:, HALF:2 * HALF], wall[s, HALF:2 * HALF, :], preferred_element_type=F32)
+        part[s] = (early[j] + rest).astype(BF16)
+        hand_over(s)
+        return c
+
+    def leaving(j, c):
+        arrived(unit(7, j), 1)
+        return second_product(j, c)
+
+    lax.fori_loop(0, 2, leaving, 0)
+
+    def second_grad(j, c):
+        @pl.when(j >= 2)
+        def _():
+            arrived(unit(7, j), 1)
+
+        add_grad(unit(7, j), 1)
+
+        @pl.when(j >= 2)
+        def _():
+            combine(unit(7, j - 2))
+
+        return c
+
+    lax.fori_loop(0, 4, second_grad, 0)
+    lax.fori_loop(heads // 2, heads, grads, 0)
 
     n_dp = gsend.shape[0]
     own_rows = prompt // n_dp
     gsend[:, 0:own_rows, :] = kg[...].reshape(n_dp, own_rows, HD)
     gsend[:, own_rows:2 * own_rows, :] = vg[...].reshape(n_dp, own_rows, HD)
 
-    def grad_copy(j):
-        return pltpu.make_async_remote_copy(
-            src_ref=gsend.at[(dp + j) % n_dp], dst_ref=grecv.at[dp], send_sem=gssem.at[j], recv_sem=grsem.at[dp],
+    def grad_send(j, c):
+        pltpu.make_async_remote_copy(
+            src_ref=gsend.at[(dp + j) % n_dp], dst_ref=grecv.at[dp], send_sem=gssem, recv_sem=grsem,
             device_id=((dp + j) % n_dp, mp), device_id_type=MESH,
-        )
-
-    def grad_send(j, c):
-        grad_copy(j).start()
+        ).start()
         return c
 
     lax.fori_loop(1, n_dp, grad_send, 0)
     grecv[dp] = gsend[dp]
+    lax.fori_loop(2, 4, second_product, 0)
+
+    def finish(i, c):
+        s = unit(i // 4, i % 4)
+
+        @pl.when(((s // 8) % 2 == core) & (s // 16 == zh))
+        def _():
+            n = index_of(s) % 8
+            far_copy(s).wait_recv()
+            out_ref[:, columns(n)] = (part[s].astype(F32) + zbuf[n].astype(F32)).astype(BF16)
+
+        return c
+
+    lax.fori_loop(0, 28, finish, 0)
+    combine(unit(7, 2))
+    combine(unit(7, 3))
 
     def drain(n, c):
         pltpu.make_async_remote_copy(
@@ -390,37 +439,23 @@
         def _():
             core_copy(s).wait_send()
 
-        @pl.when(((s // 8) % 2 == core) & (s // 16 == zh))
-        def _():
-            own_copy(s).wait()
+        @pl.when(((s // 8) % 2 == core) & (s // 16 != zh))
+        def _():
+            far_copy(s).wait_send()
 
         return c
 
     lax.fori_loop(0, n_dp, drain_parts, 0)
-
-    def grad_wait(j, c):
-        src = (dp + j) % n_dp
-        pltpu.make_async_remote_copy(
-            src_ref=gsend.at[src], dst_ref=grecv.at[src], send_sem=gssem.at[j], recv_sem=grsem.at[src],
-            device_id=(src, mp), device_id_type=MESH,
-        ).wait()
-        return c
-
-    lax.fori_loop(1, n_dp, grad_wait, 0)
-    g_out[...] = jnp.sum(grecv[...], axis=0)
-
-    def far_wait(n, c):
-        far_copy((1 - zh) * 16 + core * 8 + n).wait()
-        return c
-
-    lax.fori_loop(0, 8, far_wait, 0)
-
-
-def finish(own_ref, far_ref, g_ref, out_ref, kg_ref, vg_ref):
-    out_ref[...] = (own_ref[...].astype(F32) + far_ref[...].astype(F32)).astype(BF16)
-    n = kg_ref.shape[0]
-    kg_ref[...] = g_ref[0:n, :]
-    vg_ref[...] = g_ref[n:2 * n, :]
+    everyone = pltpu.make_async_remote_copy(
+        src_ref=gsend.at[pl.ds(0, n_dp - 1)], dst_ref=grecv.at[pl.ds(0, n_dp - 1)], send_sem=gssem, recv_sem=grsem,
+        device_id=z_peer, device_id_type=MESH,
+    )
+    everyone.wait_recv()
+    total = jnp.sum(grecv[...], axis=0)
+    kg_out[...] = total[0:own_rows, :]
+    vg_out[...] = total[own_rows:2 * own_rows, :]
+    everyone.wait_send()
+    lax.fori_loop(28, 32, finish, 0)
 
 
 def per_device(queries, keys, values, prompt_keys, prompt_values, out_weight, out_grad, lengths):
@@ -436,20 +471,22 @@
     anywhere = pl.BlockSpec(memory_space=pl.ANY)
     vmem = pl.BlockSpec(memory_space=pltpu.VMEM)
     dma = pltpu.SemaphoreType.DMA
-    own, far, grad = pl.pallas_call(
+    return pl.pallas_call(
         kernel,
         out_shape=(
-            jax.ShapeDtypeStruct((tok, 8 * UNIT), BF16),
-            jax.ShapeDtypeStruct((tok, 8 * UNIT), BF16),
-            jax.ShapeDtypeStruct((2 * own_rows, HD), F32),
+            pltpu.VMEM((tok, 8 * UNIT), BF16),
+            pltpu.VMEM((own_rows, HD), F32),
+            pltpu.VMEM((own_rows, HD), F32),
         ),
         in_specs=[anywhere] * 7 + [pl.BlockSpec(memory_space=pltpu.SMEM), vmem],
-        out_specs=(anywhere, anywhere, vmem),
+        out_specs=(vmem, vmem, vmem),
         scratch_shapes=[
             pltpu.VMEM((n_dp, width, UNIT), BF16),
             pltpu.VMEM((tok, n_dp * UNIT), BF16),
             pltpu.VMEM((n_dp, tok, UNIT), BF16),
             pltpu.VMEM((16, tok, UNIT), BF16),
+            pltpu.VMEM((8, tok, UNIT), BF16),
+            pltpu.VMEM((4, tok, UNIT), F32),
             pltpu.VMEM((prompt, HD), F32),
             pltpu.VMEM((prompt, HD), F32),
             pltpu.VMEM((n_dp, 2 * own_rows, HD), F32),
@@ -457,7 +494,7 @@
             pltpu.VMEM((tok, width), F32),
             pltpu.VMEM((tok, width), BF16),
             pltpu.VMEM((tok, width), BF16),
-            pltpu.VMEM((tok, width), BF16),
+            pltpu.VMEM((width, tok), BF16),
             pltpu.VMEM((tok, width), BF16),
             pltpu.VMEM((tok, HD), BF16),
             pltpu.VMEM((prompt + tok, HD), BF16),
@@ -472,28 +509,13 @@
             dma((16,)),
             dma((8,)),
             dma((8,)),
-            dma((8,)),
-            dma((n_dp,)),
-            dma((n_dp,)),
+            dma,
+            dma,
         ],
         compiler_params=pltpu.CompilerParams(
-            collective_id=0, has_side_effects=True, vmem_limit_bytes=62 * 1024 * 1024
+            collective_id=0, has_side_effects=True, vmem_limit_bytes=58 * 1024 * 1024
         ),
     )(queries, keys, values, prompt_keys, prompt_values, out_weight, out_grad, lengths, jnp.asarray(table))
-    block = 2 * TILE if tok % (2 * TILE) == 0 else TILE
-    wide = pl.BlockSpec((block, 8 * UNIT), lambda i: (i, 0))
-    few = pl.BlockSpec((own_rows, HD), lambda i: (0, 0))
-    return pl.pallas_call(
-        finish,
-        grid=(tok // block,),
-        out_shape=(
-            jax.ShapeDtypeStruct((tok, 8 * UNIT), BF16),
-            jax.ShapeDtypeStruct((own_rows, HD), F32),
-            jax.ShapeDtypeStruct((own_rows, HD), F32),
-        ),
-        in_specs=[wide, wide, pl.BlockSpec((2 * own_rows, HD), lambda i: (0, 0))],
-        out_specs=(wide, few, few),
-    )(own, far, grad)
 
 
 def solution(mesh):

time: 121 us -> 115 us (0.950)
  Pallas kernels: 120 us -> 111 us
  local copies, waits for them, and re-layouts: 0 us -> 2.65 us
    pallas_call x2 -> x1, Pallas kernels: 120 us -> 111 us  [per_device(): pl.pallas_call(kernel, out_shape=(pltpu.VMEM((tok, 8 * UNIT), BF16), pltp...]
    unnamed x0 -> x3, local copies, waits for them, and re-layouts: none -> 2.65 us
where the time goes in v3:
time: 115 us
  Pallas kernels  111 us (97%)
  local copies, waits for them, and re-layouts  2.65 us (2%)
    pallas_call x1, Pallas kernels, per_device(): pl.pallas_call(kernel, out_shape=(pltpu.VMEM((tok, 8 * UNIT), BF16), pltp...  111 us
    unnamed x3, local copies, waits for them, and re-layouts  2.65 us

profile of v3, /device:TPU:1, one launch (start us, length us, event | category | flops | bytes accessed | tf_op | source)
XLA Modules:
  0.0 114.7 jit_solution(8731227810017974329)
XLA Ops:
  0.6 111.4 %shard_map.112 = (bf16[640,2048]{1,0:T(8,128)(2,1)S(1)}, f32[4,128]{1,0:T(4,128)S(1)}, f32[4,128]{1,0:T(4,128)S(1)}) custom-call(bf16[640,1024]{1,0:T(8,128)(2,1)} %q_hbm.1, bf16[640,128]{1,0:T(8,128)(2,1)} %k_hbm.1, bf16[640,128]{1,0:T(8,128)(2,1)} %v_hbm.1, bf16[128,128]{1,0:T(8,128)(2,1)} %pk_hbm.1, bf16[128,128]{1,0:T(8,128)(2,1)} %pv_hbm.1, ...), custom_call_target="tpu_custom_call" | custom-call | tf_op jit(solution)/shard_map/pallas_call | solution.py:474
  112.1 1.5 %copy.15 = bf16[640,2048]{1,0:T(8,128)(2,1)} copy(bf16[640,2048]{1,0:T(8,128)(2,1)S(1)} %get-tuple-element.3) | data formatting | bytes 5242880
  113.6 0.6 copy.16
  114.2 0.6 copy.17

commit v4 on v3

--- a/solution.py
+++ b/solution.py
@@ -30,17 +30,17 @@
 STEPS = [
     [(0, 0, 0), (0, 1, 0), (0, -1, 0), (1, 0, 0)],
     [(0, 0, 1), (0, 0, -1), (0, 2, 0), (1, 0, 1)],
-    [(1, 0, -1), (1, 1, 0), (1, -1, 0), (1, 0, 2)],
-    [(0, 1, -1), (0, -1, 1), (1, -1, 1), (1, 1, -1)],
-    [(0, -1, -1), (0, 2, 1), (1, -1, -1), (1, 1, 2)],
-    [(0, 2, -1), (0, 1, 1), (1, -1, 2), (1, 1, 1)],
+    [(1, 0, -1), (1, 1, 0), (1, -1, 0), (0, 1, -1)],
+    [(0, -1, 1), (1, 0, 2), (1, -1, 1), (1, 1, -1)],
+    [(0, -1, -1), (0, 2, 1), (1, -1, -1), (1, 1, 1)],
+    [(0, 2, -1), (0, 1, 1), (1, -1, 2), (1, 1, 2)],
     [(0, 0, 2), (0, -1, 2), (1, 2, 0), (1, 2, -1)],
     [(0, 1, 2), (0, 2, 2), (1, 2, 1), (1, 2, 2)],
 ]
 TICKS = [
     [(0, 1, 0), (0, -1, 0), (1, 0, 1), (1, 0, -1)],
-    [(0, -1, 0), (0, 2, 0), (1, 0, -1), (1, 0, 2)],
-    [(0, 2, 0), (0, 1, 0), (1, 0, 2), (1, 0, 1)],
+    [(0, -1, 0), (0, 2, 0), (1, 0, -1), (1, 0, 1)],
+    [(0, 2, 0), (0, 1, 0), (1, 0, 2), (1, 0, 2)],
     [(0, 0, -1), (0, -1, 1), (1, -1, 0), (1, 1, -1)],
     [(0, 1, -1), (0, 2, 1), (1, -1, 1), (1, 1, 2)],
 ]
@@ -108,35 +108,35 @@
     def piece(s, h):
         return wall.at[s, rows(h)]
 
-    def send_own(h, peer, n):
+    def send_own(h, peer):
         pltpu.make_async_remote_copy(
-            src_ref=w_hbm.at[rows(h)], dst_ref=piece(me, h), send_sem=wsend.at[n], recv_sem=wrecv.at[me, h],
+            src_ref=w_hbm.at[rows(h)], dst_ref=piece(me, h), send_sem=wsend, recv_sem=wrecv.at[me, h],
             device_id=peer, device_id_type=MESH,
         ).start()
 
-    def send(s, h, peer, n):
+    def send(s, h, peer):
         pltpu.make_async_remote_copy(
-            src_ref=piece(s, h), dst_ref=piece(s, h), send_sem=wsend.at[n], recv_sem=wrecv.at[s, h],
+            src_ref=piece(s, h), dst_ref=piece(s, h), send_sem=wsend, recv_sem=wrecv.at[s, h],
             device_id=peer, device_id_type=MESH,
         ).start()
 
     def arrived(s, h):
         pltpu.make_async_remote_copy(
-            src_ref=piece(s, h), dst_ref=piece(s, h), send_sem=wsend.at[0], recv_sem=wrecv.at[s, h],
+            src_ref=piece(s, h), dst_ref=piece(s, h), send_sem=wsend, recv_sem=wrecv.at[s, h],
             device_id=z_peer, device_id_type=MESH,
         ).wait_recv()
 
     pl.semaphore_wait(barrier, 7)
-    send_own(0, z_peer, 0)
-    send_own(0, a_up, 1)
-    send_own(1, a_dn, 2)
-    send_own(0, b_up, 3)
-    send_own(1, b_dn, 4)
-    send_own(1, z_peer, 5)
-    send_own(1, a_up, 6)
-    send_own(0, a_dn, 7)
-    send_own(1, b_up, 8)
-    send_own(0, b_dn, 9)
+    send_own(0, z_peer)
+    send_own(0, a_up)
+    send_own(1, a_dn)
+    send_own(0, b_up)
+    send_own(1, b_dn)
+    send_own(1, z_peer)
+    send_own(1, a_up)
+    send_own(0, a_dn)
+    send_own(1, b_up)
+    send_own(0, b_dn)
     og_copy.start()
 
     t_col = lax.broadcasted_iota(jnp.int32, (tok, HD), 0)
@@ -188,31 +188,37 @@
 
         lax.fori_loop(0, heads, head, 0, unroll=2)
 
+    def both(s):
+        arrived(s, 0)
+        arrived(s, 1)
+
     attention(0)
     attention(1)
-    attention(2)
-
     arrived(slot(0, -1, 0), 0)
-    send(slot(0, -1, 0), 0, a_up, 10)
+    send(slot(0, -1, 0), 0, a_up)
     arrived(slot(0, 1, 0), 1)
-    send(slot(0, 1, 0), 1, a_dn, 11)
+    send(slot(0, 1, 0), 1, a_dn)
     other = slot(1, 0, 0)
-    arrived(other, 0)
-    send(other, 0, b_up, 12)
-    arrived(other, 1)
-    send(other, 1, b_dn, 13)
-    send(other, 1, b_up, 14)
-    send(other, 0, b_dn, 15)
-    send(other, 0, a_up, 16)
-    send(other, 1, a_dn, 17)
-    send(other, 1, a_up, 18)
-    send(other, 0, a_dn, 19)
-    attention(3)
+    for h in range(2):
+        arrived(other, h)
+        send(other, h, b_up)
+        send(other, h, b_dn)
+        send(other, h, a_up)
+        send(other, h, a_dn)
+        attention(2 + h)
+    arrived(slot(0, -1, 0), 1)
+    arrived(slot(0, 1, 0), 0)
+    for h in range(2):
+        send(slot(0, 1, 0), h, b_up)
+        send(slot(0, -1, 0), h, b_dn)
     attention(4)
-    arrived(slot(1, 0, -1), 0)
-    send(slot(1, 0, -1), 0, b_up, 20)
-    arrived(slot(1, 0, 1), 1)
-    send(slot(1, 0, 1), 1, b_dn, 21)
+    both(slot(1, 0, -1))
+    both(slot(1, 0, 1))
+    send(slot(1, 0, -1), 0, b_up)
+    send(slot(1, 0, 1), 1, b_dn)
+    for h in range(2):
+        send(slot(1, 0, 1), h, a_up)
+        send(slot(1, 0, -1), h, a_dn)
     og_copy.wait()
 
     def slot_of(step, table, j):
@@ -220,17 +226,16 @@
         return slot(kind, pick(step, [t[j][1] for t in table]), pick(step, [t[j][2] for t in table]))
 
     def tick(t):
-        n = 22 + 8 * t
         up, dn = slot_of(t, TICKS, 0), slot_of(t, TICKS, 1)
         up2, dn2 = slot_of(t, TICKS, 2), slot_of(t, TICKS, 3)
         for h in range(2):
-            send(up, h, b_up, n + h)
-            send(dn, h, b_dn, n + 2 + h)
-            send(up2, h, a_up, n + 4 + h)
-            send(dn2, h, a_dn, n + 6 + h)
+            send(up, h, b_up)
+            send(dn, h, b_dn)
+            send(up2, h, a_up)
+            send(dn2, h, a_dn)
 
     def unit(step, j):
-        i = step * 4 + jnp.where((step >= 3) & (zl == zh), (j + 2) % 4, j)
+        i = step * 4 + jnp.where((step >= 4) & (zl == zh), (j + 2) % 4, j)
         flat = [u for four in STEPS for u in four]
         return slot(pick(i, [u[0] for u in flat]), pick(i, [u[1] for u in flat]), pick(i, [u[2] for u in flat]))
 
@@ -240,14 +245,14 @@
     def core_copy(s):
         n = index_of(s)
         return pltpu.make_async_remote_copy(
-            src_ref=part.at[s], dst_ref=rbuf.at[n], send_sem=csend.at[n], recv_sem=crecv.at[n],
+            src_ref=part.at[s], dst_ref=rbuf.at[n], send_sem=csend, recv_sem=crecv.at[n],
             device_id=c_peer, device_id_type=MESH,
         )
 
     def far_copy(s):
         n = index_of(s) % 8
         return pltpu.make_async_remote_copy(
-            src_ref=part.at[s], dst_ref=zbuf.at[n], send_sem=zsend.at[n], recv_sem=zrecv.at[n],
+            src_ref=part.at[s], dst_ref=zbuf.at[n], send_sem=zsend, recv_sem=zrecv.at[n],
             device_id=far_peer, device_id_type=MESH,
         )
 
@@ -259,10 +264,11 @@
         def _():
             core_copy(s).start()
 
-    def add_grad(s, half):
-        g = og[:, columns(s)]
-        for b in range(half * HALF // UNIT, (half + 1) * HALF // UNIT):
-            w = wall[s, b * UNIT:(b + 1) * UNIT, :]
+    def add_grads(step, lo, hi):
+        four = [unit(step, j) for j in range(4)]
+        g = jnp.concatenate([og[:, columns(s)] for s in four], axis=1)
+        for b in range(lo // UNIT, hi // UNIT):
+            w = jnp.concatenate([wall[s, b * UNIT:(b + 1) * UNIT, :] for s in four], axis=1)
             acc[:, b * UNIT:(b + 1) * UNIT] += lax.dot_general(
                 g, w, (((1,), (1,)), ((), ())), preferred_element_type=F32
             )
@@ -270,8 +276,6 @@
     def process(s):
         part[s] = jnp.dot(attn[...], wall[s], preferred_element_type=F32).astype(BF16)
         hand_over(s)
-        add_grad(s, 0)
-        add_grad(s, 1)
 
     def combine(s):
         @pl.when((s // 8) % 2 == core)
@@ -284,31 +288,30 @@
             def _():
                 far_copy(s).start()
 
-    def both(s):
-        arrived(s, 0)
-        arrived(s, 1)
+    def finish(i, c):
+        s = unit(i // 4, i % 4)
+
+        @pl.when(((s // 8) % 2 == core) & (s // 16 == zh))
+        def _():
+            n = index_of(s) % 8
+            far_copy(s).wait_recv()
+            out_ref[:, columns(n)] = (part[s].astype(F32) + zbuf[n].astype(F32)).astype(BF16)
+
+        return c
 
     def step_body(step, carry):
-        @pl.when(step == 0)
-        def _():
-            arrived(slot(0, -1, 0), 1)
-            arrived(slot(0, 1, 0), 0)
-
         @pl.when(step == 1)
         def _():
             both(slot(0, 0, 1))
             both(slot(0, 0, -1))
             both(slot(0, 2, 0))
-            arrived(slot(1, 0, -1), 1)
-            arrived(slot(1, 0, 1), 0)
-            tick(0)
+            tick(1)
 
         @pl.when(step == 2)
         def _():
             both(slot(1, 1, 0))
             both(slot(1, -1, 0))
-            both(slot(1, 0, 2))
-            tick(1)
+            both(slot(0, 1, -1))
 
         @pl.when((step >= 3) & (step <= 5))
         def _():
@@ -332,7 +335,13 @@
             return c
 
         lax.fori_loop(0, 4, one, 0)
+        add_grads(step, 0, acc.shape[1])
         combine(unit(step, 3))
+
+        @pl.when(step >= 2)
+        def _():
+            lax.fori_loop(4 * (step - 2), 4 * (step - 1), finish, 0)
+
         return carry
 
     lax.fori_loop(0, 7, step_body, 0)
@@ -359,11 +368,13 @@
         s = unit(7, j)
         arrived(s, 0)
         early[j] = jnp.dot(attn[:, 0:HALF], wall[s, 0:HALF, :], preferred_element_type=F32)
-        add_grad(s, 0)
         return c
 
     lax.fori_loop(0, 4, first_half, 0)
-    lax.fori_loop(0, heads // 2, grads, 0)
+    add_grads(7, 0, HALF)
+    lax.fori_loop(0, heads // 2, grads, 0, unroll=4)
+
+    lax.fori_loop(20, 24, finish, 0)
 
     def second_product(j, c):
         s = unit(7, j)
@@ -378,21 +389,12 @@
 
     lax.fori_loop(0, 2, leaving, 0)
 
-    def second_grad(j, c):
-        @pl.when(j >= 2)
-        def _():
-            arrived(unit(7, j), 1)
-
-        add_grad(unit(7, j), 1)
-
-        @pl.when(j >= 2)
-        def _():
-            combine(unit(7, j - 2))
-
-        return c
-
-    lax.fori_loop(0, 4, second_grad, 0)
-    lax.fori_loop(heads // 2, heads, grads, 0)
+    arrived(unit(7, 2), 1)
+    arrived(unit(7, 3), 1)
+    add_grads(7, HALF, 2 * HALF)
+    combine(unit(7, 0))
+    combine(unit(7, 1))
+    lax.fori_loop(heads // 2, heads, grads, 0, unroll=4)
 
     n_dp = gsend.shape[0]
     own_rows = prompt // n_dp
@@ -410,42 +412,10 @@
     grecv[dp] = gsend[dp]
     lax.fori_loop(2, 4, second_product, 0)
 
-    def finish(i, c):
-        s = unit(i // 4, i % 4)
-
-        @pl.when(((s // 8) % 2 == core) & (s // 16 == zh))
-        def _():
-            n = index_of(s) % 8
-            far_copy(s).wait_recv()
-            out_ref[:, columns(n)] = (part[s].astype(F32) + zbuf[n].astype(F32)).astype(BF16)
-
-        return c
-
-    lax.fori_loop(0, 28, finish, 0)
+    lax.fori_loop(24, 28, finish, 0)
     combine(unit(7, 2))
     combine(unit(7, 3))
 
-    def drain(n, c):
-        pltpu.make_async_remote_copy(
-            src_ref=piece(0, 0), dst_ref=piece(0, 0), send_sem=wsend.at[n], recv_sem=wrecv.at[0, 0],
-            device_id=z_peer, device_id_type=MESH,
-        ).wait_send()
-        return c
-
-    lax.fori_loop(0, 62, drain, 0)
-
-    def drain_parts(s, c):
-        @pl.when((s // 8) % 2 != core)
-        def _():
-            core_copy(s).wait_send()
-
-        @pl.when(((s // 8) % 2 == core) & (s // 16 != zh))
-        def _():
-            far_copy(s).wait_send()
-
-        return c
-
-    lax.fori_loop(0, n_dp, drain_parts, 0)
     everyone = pltpu.make_async_remote_copy(
         src_ref=gsend.at[pl.ds(0, n_dp - 1)], dst_ref=grecv.at[pl.ds(0, n_dp - 1)], send_sem=gssem, recv_sem=grsem,
         device_id=z_peer, device_id_type=MESH,
@@ -456,6 +426,19 @@
     vg_out[...] = total[own_rows:2 * own_rows, :]
     everyone.wait_send()
     lax.fori_loop(28, 32, finish, 0)
+    for buf, sem in ((wall.at[pl.ds(0, n_dp - 1)], wsend), (rbuf, csend), (zbuf, zsend)):
+        pltpu.make_async_remote_copy(
+            src_ref=buf, dst_ref=buf, send_sem=sem, recv_sem=wrecv.at[0, 0], device_id=z_peer, device_id_type=MESH
+        ).wait_send()
+
+
+def write_out(*refs):
+    n = len(refs) // 2
+    copies = [pltpu.make_async_copy(refs[i], refs[n + i], refs[2 * n].at[i]) for i in range(n)]
+    for c in copies:
+        c.start()
+    for c in copies:
+        c.wait()
 
 
 def per_device(queries, keys, values, prompt_keys, prompt_values, out_weight, out_grad, lengths):
@@ -471,7 +454,7 @@
     anywhere = pl.BlockSpec(memory_space=pl.ANY)
     vmem = pl.BlockSpec(memory_space=pltpu.VMEM)
     dma = pltpu.SemaphoreType.DMA
-    return pl.pallas_call(
+    results = pl.pallas_call(
         kernel,
         out_shape=(
             pltpu.VMEM((tok, 8 * UNIT), BF16),
@@ -503,19 +486,26 @@
             pltpu.VMEM((tok, HD), F32),
             pltpu.VMEM((tok, HD), jnp.int32),
             dma((7,)),
-            dma((62,)),
+            dma,
             dma((n_dp, 2)),
+            dma,
             dma((16,)),
-            dma((16,)),
-            dma((8,)),
+            dma,
             dma((8,)),
             dma,
             dma,
         ],
         compiler_params=pltpu.CompilerParams(
-            collective_id=0, has_side_effects=True, vmem_limit_bytes=58 * 1024 * 1024
+            collective_id=0, has_side_effects=True, vmem_limit_bytes=60 * 1024 * 1024
         ),
     )(queries, keys, values, prompt_keys, prompt_values, out_weight, out_grad, lengths, jnp.asarray(table))
+    return pl.pallas_call(
+        write_out,
+        out_shape=tuple(jax.ShapeDtypeStruct(r.shape, r.dtype) for r in results),
+        in_specs=[vmem] * 3,
+        out_specs=(anywhere,) * 3,
+        scratch_shapes=[dma((3,))],
+    )(*(pltpu.with_memory_space_constraint(r, pltpu.VMEM) for r in results))
 
 
 def solution(mesh):

time: 115 us -> 114 us (level)
    pallas_call x1, Pallas kernels: 111 us -> 109 us  [per_device(): pl.pallas_call(kernel, out_shape=(pltpu.VMEM((tok, 8 * UNIT), BF16), pltp...]
    pallas_call x0 -> x1, Pallas kernels: none -> 1.52 us  [per_device(): pl.pallas_call(write_out, out_shape=tuple((jax.ShapeDtypeStruct(r.shape,...]
    unnamed x3 -> x4, local copies, waits for them, and re-layouts: 2.65 us -> 3.23 us
where the time goes in v4:
time: 114 us
  Pallas kernels  110 us (96%)
  local copies, waits for them, and re-layouts  3.23 us (3%)
    pallas_call x1, Pallas kernels, per_device(): pl.pallas_call(kernel, out_shape=(pltpu.VMEM((tok, 8 * UNIT), BF16), pltp...  109 us
    unnamed x4, local copies, waits for them, and re-layouts  3.23 us

profile of v4, /device:TPU:1, one launch (start us, length us, event | category | flops | bytes accessed | tf_op | source)
XLA Modules:
  0.0 113.9 jit_solution(16831757361155929165)
XLA Ops:
  0.6 108.5 %shard_map.112 = (bf16[640,2048]{1,0:T(8,128)(2,1)S(1)}, f32[4,128]{1,0:T(4,128)S(1)}, f32[4,128]{1,0:T(4,128)S(1)}) custom-call(bf16[640,1024]{1,0:T(8,128)(2,1)} %q_hbm.1, bf16[640,128]{1,0:T(8,128)(2,1)} %k_hbm.1, bf16[640,128]{1,0:T(8,128)(2,1)} %v_hbm.1, bf16[128,128]{1,0:T(8,128)(2,1)} %pk_hbm.1, bf16[128,128]{1,0:T(8,128)(2,1)} %pv_hbm.1, ...), custom_call_target="tpu_custom_call" | custom-call | tf_op jit(solution)/shard_map/pallas_call | solution.py:457
  109.2 0.0 copy-start
  109.2 1.5 %copy-done = bf16[640,2048]{1,0:T(8,128)(2,1)} copy-done((bf16[640,2048]{1,0:T(8,128)(2,1)}, bf16[640,2048]{1,0:T(8,128)(2,1)S(1)}, u32[]{:S(2)}) %copy-start) | copy-done | bytes 2621464
  110.7 0.0 copy-start.1
  110.7 1.7 %copy-done.1 = bf16[640,2048]{1,0:T(8,128)(2,1)S(1)} copy-done((bf16[640,2048]{1,0:T(8,128)(2,1)S(1)}, bf16[640,2048]{1,0:T(8,128)(2,1)}, u32[]{:S(2)}) %copy-start.1) | copy-done | bytes 2621464
  112.4 1.5 %shard_map.113 = (bf16[640,2048]{1,0:T(8,128)(2,1)}, f32[4,128]{1,0:T(4,128)}, f32[4,128]{1,0:T(4,128)}) custom-call(bf16[640,2048]{1,0:T(8,128)(2,1)S(1)} %copy-done.1, f32[4,128]{1,0:T(4,128)S(1)} %get-tuple-element.7.refs_1_, f32[4,128]{1,0:T(4,128)S(1)} %get-tuple-element.8.refs_2_), custom_call_target="tpu_custom_call" | custom-call | tf_op jit(solution)/shard_map/pallas_call | solution.py:502
Async XLA Ops:
  109.2 1.5 %copy-start = (bf16[640,2048]{1,0:T(8,128)(2,1)}, bf16[640,2048]{1,0:T(8,128)(2,1)S(1)}, u32[]{:S(2)}) copy-start(bf16[640,2048]{1,0:T(8,128)(2,1)S(1)} %get-tuple-element.6.refs_0_) | copy-start | bytes 7864324
  110.7 1.7 %copy-start.1 = (bf16[640,2048]{1,0:T(8,128)(2,1)S(1)}, bf16[640,2048]{1,0:T(8,128)(2,1)}, u32[]{:S(2)}) copy-start(bf16[640,2048]{1,0:T(8,128)(2,1)} %copy-done) | copy-start | bytes 7864324

commit v5 on v4

--- a/solution.py
+++ b/solution.py
@@ -49,7 +49,7 @@
 def kernel(
     q_hbm, k_hbm, v_hbm, pk_hbm, pv_hbm, w_hbm, og_hbm, len_ref, freq_ref,
     out_ref, kg_out, vg_out,
-    wall, og, part, rbuf, zbuf, early, kg, vg, gsend, grecv, acc, attn, qrot, prob_t, qin, kin, kall, vall, cos_t, sin_t, start_t,
+    wall, og, part, rbuf, zbuf, kg, vg, gsend, grecv, acc, attn, qrot, prob_t, qin, kin, kall, vall, cos_t, sin_t, start_t,
     in_sem, wsend, wrecv, csend, crecv, zsend, zrecv, gssem, grsem,
 ):
     tok = q_hbm.shape[0]
@@ -367,7 +367,7 @@
     def first_half(j, c):
         s = unit(7, j)
         arrived(s, 0)
-        early[j] = jnp.dot(attn[:, 0:HALF], wall[s, 0:HALF, :], preferred_element_type=F32)
+        part[s] = jnp.dot(attn[:, 0:HALF], wall[s, 0:HALF, :], preferred_element_type=F32).astype(BF16)
         return c
 
     lax.fori_loop(0, 4, first_half, 0)
@@ -379,7 +379,7 @@
     def second_product(j, c):
         s = unit(7, j)
         rest = jnp.dot(attn[:, HALF:2 * HALF], wall[s, HALF:2 * HALF, :], preferred_element_type=F32)
-        part[s] = (early[j] + rest).astype(BF16)
+        part[s] = (part[s].astype(F32) + rest).astype(BF16)
         hand_over(s)
         return c
 
@@ -469,7 +469,6 @@
             pltpu.VMEM((n_dp, tok, UNIT), BF16),
             pltpu.VMEM((16, tok, UNIT), BF16),
             pltpu.VMEM((8, tok, UNIT), BF16),
-            pltpu.VMEM((4, tok, UNIT), F32),
             pltpu.VMEM((prompt, HD), F32),
             pltpu.VMEM((prompt, HD), F32),
             pltpu.VMEM((n_dp, 2 * own_rows, HD), F32),
@@ -496,7 +495,7 @@
             dma,
         ],
         compiler_params=pltpu.CompilerParams(
-            collective_id=0, has_side_effects=True, vmem_limit_bytes=60 * 1024 * 1024
+            collective_id=0, has_side_effects=True, vmem_limit_bytes=58 * 1024 * 1024
         ),
     )(queries, keys, values, prompt_keys, prompt_values, out_weight, out_grad, lengths, jnp.asarray(table))
     return pl.pallas_call(

time: 114 us -> 111 us (0.974)
  local copies, waits for them, and re-layouts: 3.23 us -> 0 us
    unnamed x4 -> x0, local copies, waits for them, and re-layouts: 3.23 us -> none
where the time goes in v5:
time: 111 us
  Pallas kernels  110 us (99%)
    pallas_call x1, Pallas kernels, per_device(): pl.pallas_call(kernel, out_shape=(pltpu.VMEM((tok, 8 * UNIT), BF16), pltp...  109 us

profile of v5, /device:TPU:1, one launch (start us, length us, event | category | flops | bytes accessed | tf_op | source)
XLA Modules:
  0.0 110.7 jit_solution(13380815206338353348)
XLA Ops:
  0.6 108.5 %shard_map.112 = (bf16[640,2048]{1,0:T(8,128)(2,1)S(1)}, f32[4,128]{1,0:T(4,128)S(1)}, f32[4,128]{1,0:T(4,128)S(1)}) custom-call(bf16[640,1024]{1,0:T(8,128)(2,1)} %q_hbm.1, bf16[640,128]{1,0:T(8,128)(2,1)} %k_hbm.1, bf16[640,128]{1,0:T(8,128)(2,1)} %v_hbm.1, bf16[128,128]{1,0:T(8,128)(2,1)} %pk_hbm.1, bf16[128,128]{1,0:T(8,128)(2,1)} %pv_hbm.1, ...), custom_call_target="tpu_custom_call" | custom-call | tf_op jit(solution)/shard_map/pallas_call | solution.py:457
  109.2 1.5 %shard_map.113 = (bf16[640,2048]{1,0:T(8,128)(2,1)}, f32[4,128]{1,0:T(4,128)}, f32[4,128]{1,0:T(4,128)}) custom-call(bf16[640,2048]{1,0:T(8,128)(2,1)S(1)} %get-tuple-element.6.refs_0_, f32[4,128]{1,0:T(4,128)S(1)} %get-tuple-element.7.refs_1_, f32[4,128]{1,0:T(4,128)S(1)} %get-tuple-element.8.refs_2_), custom_call_target="tpu_custom_call" | custom-call | tf_op jit(solution)/shard_map/pallas_call | solution.py:501

commit v6 on v5

--- a/solution.py
+++ b/solution.py
@@ -125,6 +125,13 @@
             src_ref=piece(s, h), dst_ref=piece(s, h), send_sem=wsend, recv_sem=wrecv.at[s, h],
             device_id=z_peer, device_id_type=MESH,
         ).wait_recv()
+
+    def quarter_copy(s, r, c, peer):
+        quarter = wall.at[s, rows(r), pl.ds(c * HD, HD)]
+        return pltpu.make_async_remote_copy(
+            src_ref=quarter, dst_ref=quarter, send_sem=wsend, recv_sem=wrecv.at[s, 2 * c + r],
+            device_id=peer, device_id_type=MESH,
+        )
 
     pl.semaphore_wait(barrier, 7)
     send_own(0, z_peer)
@@ -234,6 +241,26 @@
             send(up2, h, a_up)
             send(dn2, h, a_dn)
 
+    def last_tick():
+        on_b = ((slot_of(4, TICKS, 0), b_up), (slot_of(4, TICKS, 1), b_dn))
+        on_a = ((slot_of(4, TICKS, 2), a_up), (slot_of(4, TICKS, 3), a_dn))
+
+        def go(leave, stay):
+            for c in range(2):
+                for r in range(2):
+                    for s, peer in leave:
+                        quarter_copy(s, r, c, peer).start()
+                for s, peer in stay:
+                    send(s, c, peer)
+
+        @pl.when(zl == zh)
+        def _():
+            go(on_a, on_b)
+
+        @pl.when(zl != zh)
+        def _():
+            go(on_b, on_a)
+
     def unit(step, j):
         i = step * 4 + jnp.where((step >= 4) & (zl == zh), (j + 2) % 4, j)
         flat = [u for four in STEPS for u in four]
@@ -242,27 +269,30 @@
     def index_of(s):
         return (s // 16) * 8 + ((s // 4) % 2) * 4 + s % 4
 
-    def core_copy(s):
+    def part_of(c):
+        return pl.ds(0, UNIT) if c is None else pl.ds(c * HD, HD)
+
+    def core_copy(s, c=None):
         n = index_of(s)
         return pltpu.make_async_remote_copy(
-            src_ref=part.at[s], dst_ref=rbuf.at[n], send_sem=csend, recv_sem=crecv.at[n],
-            device_id=c_peer, device_id_type=MESH,
+            src_ref=part.at[s, :, part_of(c)], dst_ref=rbuf.at[n, :, part_of(c)], send_sem=csend,
+            recv_sem=crecv.at[n, c or 0], device_id=c_peer, device_id_type=MESH,
         )
 
-    def far_copy(s):
+    def far_copy(s, c=None):
         n = index_of(s) % 8
         return pltpu.make_async_remote_copy(
-            src_ref=part.at[s], dst_ref=zbuf.at[n], send_sem=zsend, recv_sem=zrecv.at[n],
-            device_id=far_peer, device_id_type=MESH,
+            src_ref=part.at[s, :, part_of(c)], dst_ref=zbuf.at[n, :, part_of(c)], send_sem=zsend,
+            recv_sem=zrecv.at[n, c or 0], device_id=far_peer, device_id_type=MESH,
         )
 
     def columns(n):
         return pl.ds(pl.multiple_of(n * UNIT, UNIT), UNIT)
 
-    def hand_over(s):
+    def hand_over(s, c=None):
         @pl.when((s // 8) % 2 != core)
         def _():
-            core_copy(s).start()
+            core_copy(s, c).start()
 
     def add_grads(step, lo, hi):
         four = [unit(step, j) for j in range(4)]
@@ -277,27 +307,33 @@
         part[s] = jnp.dot(attn[...], wall[s], preferred_element_type=F32).astype(BF16)
         hand_over(s)
 
-    def combine(s):
+    def combine(s, c=None):
         @pl.when((s // 8) % 2 == core)
         def _():
             n = index_of(s)
-            core_copy(s).wait_recv()
-            part[s] = (part[s].astype(F32) + rbuf[n].astype(F32)).astype(BF16)
+            core_copy(s, c).wait_recv()
+            p = part_of(c)
+            part[s, :, p] = (part[s, :, p].astype(F32) + rbuf[n, :, p].astype(F32)).astype(BF16)
 
             @pl.when(s // 16 != zh)
             def _():
-                far_copy(s).start()
-
-    def finish(i, c):
-        s = unit(i // 4, i % 4)
-
+                far_copy(s, c).start()
+
+    def finish_of(s, c=None):
         @pl.when(((s // 8) % 2 == core) & (s // 16 == zh))
         def _():
             n = index_of(s) % 8
-            far_copy(s).wait_recv()
-            out_ref[:, columns(n)] = (part[s].astype(F32) + zbuf[n].astype(F32)).astype(BF16)
-
-        return c
+            far_copy(s, c).wait_recv()
+            p = part_of(c)
+            at = 0 if c is None else c * HD
+            wide = UNIT if c is None else HD
+            out_ref[:, pl.ds(pl.multiple_of(n * UNIT + at, HD), wide)] = (
+                part[s, :, p].astype(F32) + zbuf[n, :, p].astype(F32)
+            ).astype(BF16)
+
+    def finish(i, carry):
+        finish_of(unit(i // 4, i % 4))
+        return carry
 
     def step_body(step, carry):
         @pl.when(step == 1)
@@ -317,7 +353,14 @@
         def _():
             for j in range(4):
                 both(unit(step, j))
+
+        @pl.when((step >= 3) & (step <= 4))
+        def _():
             tick(step - 1)
+
+        @pl.when(step == 5)
+        def _():
+            last_tick()
 
         def one(j, c):
             s = unit(step, j)
@@ -364,17 +407,28 @@
         vg[...] += lax.dot_general(p, g, nn, preferred_element_type=F32)
         return c
 
+    def last_arrived(j, r, c):
+        quarter_copy(unit(7, j), r, c, z_peer).wait_recv()
+
+    def leaving(c):
+        def one(j, carry):
+            s = unit(7, j)
+            if c == 0:
+                last_arrived(j, 0, 0)
+            last_arrived(j, 1, c)
+            part[s, :, part_of(c)] = jnp.dot(
+                attn[...], wall[s, :, c * HD:(c + 1) * HD], preferred_element_type=F32
+            ).astype(BF16)
+            hand_over(s, c)
+            return carry
+
+        lax.fori_loop(0, 2, one, 0)
+
     def first_half(j, c):
         s = unit(7, j)
         arrived(s, 0)
         part[s] = jnp.dot(attn[:, 0:HALF], wall[s, 0:HALF, :], preferred_element_type=F32).astype(BF16)
         return c
-
-    lax.fori_loop(0, 4, first_half, 0)
-    add_grads(7, 0, HALF)
-    lax.fori_loop(0, heads // 2, grads, 0, unroll=4)
-
-    lax.fori_loop(20, 24, finish, 0)
 
     def second_product(j, c):
         s = unit(7, j)
@@ -383,17 +437,21 @@
         hand_over(s)
         return c
 
-    def leaving(j, c):
-        arrived(unit(7, j), 1)
-        return second_product(j, c)
-
-    lax.fori_loop(0, 2, leaving, 0)
-
+    leaving(0)
+    lax.fori_loop(2, 4, first_half, 0)
+    combine(unit(7, 0), 0)
+    combine(unit(7, 1), 0)
+    lax.fori_loop(20, 24, finish, 0)
+    last_arrived(0, 0, 1)
+    last_arrived(1, 0, 1)
+    add_grads(7, 0, HALF)
+    lax.fori_loop(0, heads // 2, grads, 0, unroll=4)
+    leaving(1)
     arrived(unit(7, 2), 1)
     arrived(unit(7, 3), 1)
     add_grads(7, HALF, 2 * HALF)
-    combine(unit(7, 0))
-    combine(unit(7, 1))
+    combine(unit(7, 0), 1)
+    combine(unit(7, 1), 1)
     lax.fori_loop(heads // 2, heads, grads, 0, unroll=4)
 
     n_dp = gsend.shape[0]
@@ -425,7 +483,13 @@
     kg_out[...] = total[0:own_rows, :]
     vg_out[...] = total[own_rows:2 * own_rows, :]
     everyone.wait_send()
-    lax.fori_loop(28, 32, finish, 0)
+
+    def last_finish(j, carry):
+        finish_of(unit(7, j), 0)
+        finish_of(unit(7, j), 1)
+        return carry
+
+    lax.fori_loop(2, 4, last_finish, 0)
     for buf, sem in ((wall.at[pl.ds(0, n_dp - 1)], wsend), (rbuf, csend), (zbuf, zsend)):
         pltpu.make_async_remote_copy(
             src_ref=buf, dst_ref=buf, send_sem=sem, recv_sem=wrecv.at[0, 0], device_id=z_peer, device_id_type=MESH
@@ -486,11 +550,11 @@
             pltpu.VMEM((tok, HD), jnp.int32),
             dma((7,)),
             dma,
-            dma((n_dp, 2)),
+            dma((n_dp, 4)),
             dma,
-            dma((16,)),
+            dma((16, 2)),
             dma,
-            dma((8,)),
+            dma((8, 2)),
             dma,
             dma,
         ],

time: 111 us -> 109 us (0.982)
    pallas_call x1, Pallas kernels: 109 us -> 107 us  [per_device(): pl.pallas_call(kernel, out_shape=(pltpu.VMEM((tok, 8 * UNIT), BF16), pltp...]
where the time goes in v6:
time: 109 us
  Pallas kernels  109 us (100%)
    pallas_call x1, Pallas kernels, per_device(): pl.pallas_call(kernel, out_shape=(pltpu.VMEM((tok, 8 * UNIT), BF16), pltp...  107 us

profile of v6, /device:TPU:1, one launch (start us, length us, event | category | flops | bytes accessed | tf_op | source)
XLA Modules:
  0.0 109.3 jit_solution(10313991549374446134)
XLA Ops:
  0.6 107.0 %shard_map.112 = (bf16[640,2048]{1,0:T(8,128)(2,1)S(1)}, f32[4,128]{1,0:T(4,128)S(1)}, f32[4,128]{1,0:T(4,128)S(1)}) custom-call(bf16[640,1024]{1,0:T(8,128)(2,1)} %q_hbm.1, bf16[640,128]{1,0:T(8,128)(2,1)} %k_hbm.1, bf16[640,128]{1,0:T(8,128)(2,1)} %v_hbm.1, bf16[128,128]{1,0:T(8,128)(2,1)} %pk_hbm.1, bf16[128,128]{1,0:T(8,128)(2,1)} %pv_hbm.1, ...), custom_call_target="tpu_custom_call" | custom-call | tf_op jit(solution)/shard_map/pallas_call | solution.py:521
  107.6 1.5 %shard_map.113 = (bf16[640,2048]{1,0:T(8,128)(2,1)}, f32[4,128]{1,0:T(4,128)}, f32[4,128]{1,0:T(4,128)}) custom-call(bf16[640,2048]{1,0:T(8,128)(2,1)S(1)} %get-tuple-element.6.refs_0_, f32[4,128]{1,0:T(4,128)S(1)} %get-tuple-element.7.refs_1_, f32[4,128]{1,0:T(4,128)S(1)} %get-tuple-element.8.refs_2_), custom_call_target="tpu_custom_call" | custom-call | tf_op jit(solution)/shard_map/pallas_call | solution.py:565

commit v7 on v6

--- a/solution.py
+++ b/solution.py
@@ -261,10 +261,18 @@
         def _():
             go(on_b, on_a)
 
+    order = []
+    for step, four in enumerate(STEPS):
+        here = [slot(*u) for u in four]
+        if step >= 4:
+            here = [jnp.where(zl == zh, here[(j + 2) % 4], here[j]) for j in range(4)]
+        order.extend(here)
+
     def unit(step, j):
-        i = step * 4 + jnp.where((step >= 4) & (zl == zh), (j + 2) % 4, j)
-        flat = [u for four in STEPS for u in four]
-        return slot(pick(i, [u[0] for u in flat]), pick(i, [u[1] for u in flat]), pick(i, [u[2] for u in flat]))
+        if isinstance(step, int):
+            four = order[4 * step:4 * step + 4]
+            return four[j] if isinstance(j, int) else pick(j, four)
+        return pick(step * 4 + j, order)
 
     def index_of(s):
         return (s // 16) * 8 + ((s // 4) % 2) * 4 + s % 4

time: 109 us -> 109 us (level)
  no operation moved by 1% of the time
where the time goes in v7:
time: 109 us
  Pallas kernels  108 us (99%)
    pallas_call x1, Pallas kernels, per_device(): pl.pallas_call(kernel, out_shape=(pltpu.VMEM((tok, 8 * UNIT), BF16), pltp...  106 us

profile of v7, /device:TPU:1, one launch (start us, length us, event | category | flops | bytes accessed | tf_op | source)
XLA Modules:
  0.0 108.6 jit_solution(14400622034419110256)
XLA Ops:
  0.6 106.5 %shard_map.112 = (bf16[640,2048]{1,0:T(8,128)(2,1)S(1)}, f32[4,128]{1,0:T(4,128)S(1)}, f32[4,128]{1,0:T(4,128)S(1)}) custom-call(bf16[640,1024]{1,0:T(8,128)(2,1)} %q_hbm.1, bf16[640,128]{1,0:T(8,128)(2,1)} %k_hbm.1, bf16[640,128]{1,0:T(8,128)(2,1)} %v_hbm.1, bf16[128,128]{1,0:T(8,128)(2,1)} %pk_hbm.1, bf16[128,128]{1,0:T(8,128)(2,1)} %pv_hbm.1, ...), custom_call_target="tpu_custom_call" | custom-call | tf_op jit(solution)/shard_map/pallas_call | solution.py:529
  107.1 1.5 %shard_map.113 = (bf16[640,2048]{1,0:T(8,128)(2,1)}, f32[4,128]{1,0:T(4,128)}, f32[4,128]{1,0:T(4,128)}) custom-call(bf16[640,2048]{1,0:T(8,128)(2,1)S(1)} %get-tuple-element.6.refs_0_, f32[4,128]{1,0:T(4,128)S(1)} %get-tuple-element.7.refs_1_, f32[4,128]{1,0:T(4,128)S(1)} %get-tuple-element.8.refs_2_), custom_call_target="tpu_custom_call" | custom-call | tf_op jit(solution)/shard_map/pallas_call | solution.py:573
